TPU v7x, 512 devices: a whole 4x8x8 slice. The times are simulated.
512 devices in a mesh: wide: 32 (over x, y), grp: 16 (over z, core).
Axes of the slice: x: 4, y: 8, z: 8, core: 2. Of those that a mesh axis runs over, the one named last changes fastest.
Arguments:
- source: float32 [256, 256, 128], P('wide', 'grp'), may hold values from -6 to 6
- conductivity: float32 [256, 256, 128], P('wide', 'grp'), may hold values from 0.02 to 0.5
- ice_cells: int32 [256, 256], P('wide', 'grp'), may hold values from 1 to 128, as said below
Outputs:
- pressure: float32 [256, 256, 128], P('wide', 'grp')
Inputs may be any that keep to these rules, and one draw needn't show every extreme that they name: Column (x, y) holds ice in its lowest ice_cells[x, y] cells; some column is 128 cells high.
All inputs are finite; a program needn't handle non-finite values.
Results may differ from a plain program's by a relative error of at most 0.0001.
Values sent between devices are 32-bit elements; how exact they have to be, the bound alone decides.
No kernel may reach another device: no remote copies, remote signals or barrier semaphores. Data moves between devices by JAX's collectives and lax.ppermute only.
A program may use at most 64 MiB of HBM per device.

v0:
```python
import functools

import jax
import jax.numpy as jnp
from jax import lax
from jax.experimental import pallas as pl
from jax.experimental.pallas import tpu as pltpu
from jax.sharding import Mesh
from jax.sharding import PartitionSpec as P

ITERS = 6

cheb_center = (2.0 + 0.3) / 2.0
cheb_radius = (2.0 - 0.3) / 2.0
first_ratio = cheb_radius / cheb_center
second_ratio = 1.0 / (2.0 * cheb_center / cheb_radius - first_ratio)
carry_weight = second_ratio * first_ratio
fresh_weight = 2.0 * second_ratio / cheb_radius
inverse_center = 1.0 / cheb_center

F32 = jnp.float32
BX, BY, BZ = 8, 16, 128
PACK = 2 * BX + 1
NS, NC = 6, 7
SIDE = NS + NC + 1
STRIP = 2 * SIDE + PACK
HALF = 4
EX, EY = 3 * BX, 3 * BY
MX, MY = EX // 2, EY // 2
TX, TY = 12, 32
X0, Y0 = 6, 8
BLOCK = 16
ROWS = 5


def lane_index(shape):
    return lax.broadcasted_iota(jnp.int32, shape, len(shape) - 1)


def pair_weight(factor, coef, neighbour):
    total = coef + neighbour
    return (2.0 * factor) * coef * neighbour / jnp.where(total > 0.0, total, 1.0)


def shift(value, amount, axis):
    return pltpu.roll(value, amount % value.shape[axis], axis)


def operate(before, value, after, weight_x, weight_x_before, weight_y, weight_z, diagonal, active, step_z):
    coupled = weight_x * after + weight_x_before * before
    coupled = coupled + weight_y * shift(value, -1, 0)
    coupled = coupled + shift(weight_y * value, 1, 0)
    coupled = coupled + weight_z * shift(value, -step_z, 1)
    coupled = coupled + shift(weight_z * value, step_z, 1)
    return active * (diagonal * value - coupled)


def pair_lanes(value, step, combine):
    lanes = lane_index(value.shape)
    other = jnp.where((lanes & step) == 0, shift(value, -step, 1), shift(value, step, 1))
    return combine(value, other)


def loop(low, high, step, body):
    assert (high - low) % step == 0

    def turn(i, carry):
        for k in range(step):
            body(low + i * step + k, k)
        return carry

    lax.fori_loop(0, (high - low) // step, turn, 0)


def face_weights(factor, coef_ref, wx_ref, wy_ref, wz_ref, low, high, step, step_z):
    def body(x, slot):
        coef = coef_ref[x]
        lanes = lane_index(coef.shape)
        wx_ref[x + 1] = pair_weight(factor, coef, coef_ref[x + 1])
        wy_ref[x] = pair_weight(factor, coef, shift(coef, -1, 0))
        weight = pair_weight(factor, coef, shift(coef, -step_z, 1))
        wz_ref[x] = jnp.where(lanes >= BZ - step_z, 0.0, weight)

    wx_ref[low] = pair_weight(factor, coef_ref[low - 1], coef_ref[low])
    loop(low, high, step, body)


def diagonal_of(factor, x, coef_ref, wx_ref, wy_ref, wz_ref, step_z):
    coef = coef_ref[x]
    lanes = lane_index(coef.shape)
    weight_y, weight_z = wy_ref[x], wz_ref[x]
    top = jnp.where(lanes >= BZ - step_z, factor * coef, weight_z)
    total = wx_ref[x + 1] + wx_ref[x] + weight_y + shift(weight_y, 1, 0)
    return total + top + shift(weight_z, step_z, 1)


def inverse_of(diagonal):
    return 1.0 / jnp.where(diagonal > 0.0, diagonal, 1.0)


def strip_kernel(own_ref, before_ref, after_ref, up_ref, down_ref):
    for i in range(STRIP):
        if i < SIDE:
            row = before_ref[i]
        elif i < SIDE + PACK:
            row = own_ref[i - SIDE]
        else:
            row = after_ref[i - SIDE - PACK]
        k, part = STRIP + i // 2, slice(HALF * (i % 2), HALF * (i % 2 + 1))
        up_ref[i] = row[BY - 8:]
        up_ref[k, part] = row[BY - 8 - HALF:BY - 8]
        down_ref[i] = row[:8]
        down_ref[k, part] = row[8:8 + HALF]


def local_kernel(
    own_ref, before_ref, after_ref, up_ref, down_ref,
    fan_ref, edge_ref,
    load1_ref, active1_ref, wx1_ref, wy1_ref, wz1_ref, diag1_ref, inv1_ref, smooth1_ref,
    load0_ref, active0_ref, wx0_ref, wy0_ref, wz0_ref, diag0_ref, inv0_ref, smooth0_ref,
    source, coef, active, wx, wy, wz, diag, inv, update, smooth, coef1, update1, pairs, tops, coarse,
):
    edge_rows = jnp.zeros((8 - HALF, BZ), F32)

    def extended(i):
        if i < SIDE:
            own = before_ref[i]
        elif i < SIDE + PACK:
            own = own_ref[i - SIDE]
        else:
            own = after_ref[i - SIDE - PACK]
        k, part = STRIP + i // 2, slice(HALF * (i % 2), HALF * (i % 2 + 1))
        return jnp.concatenate(
            [edge_rows, up_ref[k, part], up_ref[i], own, down_ref[i], down_ref[k, part], edge_rows], 0
        )

    middle = SIDE
    last = SIDE + PACK
    for i in range(NS):
        source[BX - NS + i] = extended(i)
        source[2 * BX + i] = extended(last + i)
    for i in range(NC):
        coef[BX - NC + i] = extended(NS + i)
        coef[2 * BX + i] = extended(last + NS + i)
    for i in range(BX):
        source[BX + i] = extended(middle + i)
        coef[BX + i] = extended(middle + BX + i)
    for j, i in enumerate((SIDE - 1, last - 1, STRIP - 1)):
        columns = extended(i)
        for x in range(BX):
            active[j * BX + x] = jnp.broadcast_to(columns[:, x:x + 1], (EY, BZ))

    low0, high0 = BX - NS, 2 * BX + NS
    low1, high1 = low0 // 2 + 1, high0 // 2 - 1

    def middle_tops(x, slot):
        pairs[slot] = jnp.maximum(active[2 * x], active[2 * x + 1])
        value = jnp.maximum(
            pairs[slot, pl.ds(0, MY, stride=2), :], pairs[slot, pl.ds(1, MY, stride=2), :]
        )
        tops[x] = value
        layer = (lane_index((MY, BZ)) & ~1).astype(F32)
        active1_ref[x] = (layer < value).astype(F32)

    loop(0, MX, 2, middle_tops)

    def fine_mask(x, slot):
        layer = lane_index((EY, BZ)).astype(F32)
        mask = (layer < active[x]).astype(F32)
        active[x] = mask
        source[x] = mask * source[x]

    loop(low0, high0, 2, fine_mask)

    face_weights(1.0, coef, wx, wy, wz, low0, high0, 2, 1)

    def fine_start(x, slot):
        diagonal = diagonal_of(1.0, x, coef, wx, wy, wz, 1)
        inverse = inverse_of(diagonal)
        diag[x] = diagonal
        inv[x] = inverse
        update[x] = source[x] * (inverse * inverse_center)

    loop(low0, high0, 2, fine_start)

    def fine_operate(ref, x):
        return operate(ref[x - 1], ref[x], ref[x + 1], wx[x + 1], wx[x], wy[x], wz[x], diag[x], active[x], 1)

    def fine_finish(x, slot):
        residual = source[x] - fine_operate(update, x)
        first = update[x]
        smooth[x] = first + (carry_weight * first + fresh_weight * residual * inv[x])

    loop(low0 + 1, high0 - 1, 2, fine_finish)

    def keep(i, slot):
        for kept, ref in (
            (load0_ref, source), (active0_ref, active), (wy0_ref, wy), (wz0_ref, wz),
            (diag0_ref, diag), (inv0_ref, inv), (smooth0_ref, smooth),
        ):
            kept[i] = ref[X0 + i, Y0:Y0 + TY, :]
        wx0_ref[i] = wx[X0 + i, Y0:Y0 + TY, :]

    loop(0, TX, 2, keep)

    def restrict(value, slot):
        pairs[slot] = pair_lanes(value, 1, jnp.add)
        return pairs[slot, pl.ds(0, MY, stride=2), :] + pairs[slot, pl.ds(1, MY, stride=2), :]

    def middle_coef(x, slot):
        coef1[x] = restrict(coef[2 * x] + coef[2 * x + 1], slot) * 0.125

    loop(low1 - 1, high1 + 1, 2, middle_coef)

    def middle_load(x, slot):
        left = source[2 * x] - fine_operate(smooth, 2 * x)
        right = source[2 * x + 1] - fine_operate(smooth, 2 * x + 1)
        load1_ref[x] = restrict(left + right, slot)

    loop(low1, high1, 2, middle_load)

    face_weights(2.0, coef1, wx1_ref, wy1_ref, wz1_ref, low1, high1, 4, 2)

    def middle_start(x, slot):
        diagonal = diagonal_of(2.0, x, coef1, wx1_ref, wy1_ref, wz1_ref, 2)
        inverse = inverse_of(diagonal)
        diag1_ref[x] = diagonal
        inv1_ref[x] = inverse
        update1[x] = load1_ref[x] * (inverse * inverse_center)

    loop(low1, high1, 4, middle_start)

    def middle_operate(ref, x):
        return operate(
            ref[x - 1], ref[x], ref[x + 1], wx1_ref[x + 1], wx1_ref[x], wy1_ref[x], wz1_ref[x],
            diag1_ref[x], active1_ref[x], 2,
        )

    def middle_finish(x, slot):
        residual = load1_ref[x] - middle_operate(update1, x)
        first = update1[x]
        smooth1_ref[x] = first + (carry_weight * first + fresh_weight * residual * inv1_ref[x])

    loop(low1 + 1, high1 - 1, 3, middle_finish)
    for i in range(2):
        edge_ref[i] = smooth1_ref[MX // 2 - 1 + i]

    first_x, first_y = MX // 3, MY // 3
    rows = []
    for part in range(2):
        for cx in range(2):
            if part == 0:
                total = sum(
                    load1_ref[x] - middle_operate(smooth1_ref, x)
                    for x in (first_x + 2 * cx, first_x + 2 * cx + 1)
                )
            else:
                total = (coef1[first_x + 2 * cx] + coef1[first_x + 2 * cx + 1]) * 0.125
            coarse[...] = pair_lanes(total, 2, jnp.add)
            value = (
                coarse[pl.ds(first_y, 4, stride=2), :] + coarse[pl.ds(first_y + 1, 4, stride=2), :]
            )
            rows.append(jnp.concatenate([value[i:i + 1] for i in range(4)], 1))
    spread = jnp.concatenate(rows + [jnp.zeros((4, 4 * BZ), F32)], 0)
    entry = lax.broadcasted_iota(jnp.int32, (4 * BZ, BZ), 0)
    lanes = lane_index((4 * BZ, BZ))
    chosen = (entry // BZ == lanes // 32) & (entry % BZ == (lanes % 32) * 4)
    packed = jnp.dot(
        spread, chosen.astype(F32), precision=lax.Precision.HIGHEST, preferred_element_type=F32
    )
    lanes = lane_index((1, BZ))
    top_row = jnp.zeros((1, BZ), F32)
    for cx in range(2):
        coarse[...] = jnp.maximum(tops[first_x + 2 * cx], tops[first_x + 2 * cx + 1])
        value = jnp.maximum(
            coarse[pl.ds(first_y, 4, stride=2), :], coarse[pl.ds(first_y + 1, 4, stride=2), :]
        )
        for cy in range(4):
            top_row = jnp.where(lanes // 16 == 2 * cy + cx, value[cy:cy + 1], top_row)
    block = [packed[i:i + 1] for i in range(4)] + [top_row]
    pattern = jnp.concatenate(block * 8, 0)

    def fan(i, carry):
        fan_ref[pl.ds(pl.multiple_of(i * 8 * ROWS, 8), 8 * ROWS), :] = pattern
        return carry

    lax.fori_loop(0, fan_ref.shape[0] // (8 * ROWS), fan, 0)


def finish_kernel(
    wide, deep, mine_ref, other_ref, even_ref, odd_ref,
    load1_ref, active1_ref, wx1_ref, wy1_ref, wz1_ref, diag1_ref, inv1_ref, smooth1_ref,
    load0_ref, active0_ref, wx0_ref, wy0_ref, wz0_ref, diag0_ref, inv0_ref, smooth0_ref,
    out_ref,
    coef, active, wx, wy, wz, diag, residual, image, slope, direction, solution, wanted, spread,
    guess1, update1, second1, children, guess0, update0, second0,
):
    count = 2 * wide
    vector = (deep, BZ)
    lanes = lane_index((BLOCK, deep, BZ))
    zero = jnp.zeros(vector, F32)
    pad = 2

    def pair(first, second):
        return jnp.stack([first, second], 1)

    def y_after(value):
        turned = shift(value, -32, 3)
        first, second = turned[:, 0], turned[:, 1]
        inside = lanes < 96
        return pair(jnp.where(inside, first, second), jnp.where(inside, second, shift(first, -1, 1)))

    def y_before(value):
        turned = shift(value, 32, 3)
        first, second = turned[:, 0], turned[:, 1]
        inside = lanes >= 32
        return pair(jnp.where(inside, first, shift(second, 1, 1)), jnp.where(inside, second, first))

    for ref, spare in ((residual, (*range(pad), *range(count + pad, count + 2 * pad))), (image, (count,)), (slope, (count,))):
        for x in spare:
            ref[x] = jnp.zeros((2, *vector), F32)

    stride = deep * ROWS
    flat = lane_index(vector)
    low = (flat & 16) == 0
    layer = ((flat & 31) * 4).astype(F32)

    def unpack(refs):
        def body(w, slot):
            for c in range(2):
                top, *rows = (
                    refs[c][pl.ds(w * stride + k, deep, stride=ROWS), :] for k in (4, 0, 1, 2, 3)
                )
                tall = (
                    jnp.where(low, top, shift(top, 16, 1)), jnp.where(low, shift(top, -16, 1), top)
                )
                for i in range(2):
                    residual[2 * w + i + pad, c] = rows[i]
                    coef[2 * w + i, c] = rows[2 + i]
                    active[2 * w + i, c] = (layer < tall[i]).astype(F32)

        loop(0, wide, 2, body)

    own_core = lax.axis_index("core")

    @pl.when(own_core == 0)
    def _():
        unpack((mine_ref, other_ref))

    @pl.when(own_core == 1)
    def _():
        unpack((other_ref, mine_ref))

    lanes4 = lane_index((BLOCK, 2, deep, BZ))
    highest = (lanes4 & 31) == 31
    shape4 = (BLOCK, 2, deep, BZ)
    last_y = (
        (lanes4 >= 96)
        & (lax.broadcasted_iota(jnp.int32, shape4, 1) == 1)
        & (lax.broadcasted_iota(jnp.int32, shape4, 2) == deep - 1)
    )

    def coarse_weight(a, b):
        return 8.0 * a * b / (a + b)

    coef[count] = jnp.zeros((2, *vector), F32)
    active[count] = jnp.zeros((2, *vector), F32)
    wx[0] = jnp.zeros((2, *vector), F32)

    def setup(i, face):
        x = i * BLOCK
        coefs, masks = coef[pl.ds(x, BLOCK + 1)], active[pl.ds(x, BLOCK + 1)]
        here, mask = coefs[:BLOCK], masks[:BLOCK]
        after = coarse_weight(here, coefs[1:])
        before = jnp.concatenate([face, after[:-1]], 0)
        beside = jnp.where(last_y, 0.0, coarse_weight(here, y_after(here)))
        above = coarse_weight(here, shift(here, -1, 3))
        inner = jnp.where(highest, 0.0, above)
        top = jnp.where(highest, 4.0 * here, above)
        total = after + before + beside + y_before(beside) + top + shift(inner, 1, 3)
        diag[pl.ds(x, BLOCK)] = mask * total
        wx[pl.ds(x + 1, BLOCK)] = after * (mask * masks[1:])
        wy[pl.ds(x, BLOCK)] = beside * (mask * y_after(mask))
        wz[pl.ds(x, BLOCK)] = inner * (mask * shift(mask, -1, 3))
        return after[-1:]

    lax.fori_loop(0, count // BLOCK, setup, jnp.zeros((1, 2, *vector), F32))

    def whole(total):
        return jnp.sum(jnp.sum(total, axis=0, keepdims=True), axis=1, keepdims=True)

    def fold(total, value):
        return total + jnp.sum(value, axis=(0, 1))

    first = 2 * lax.axis_index("wide")
    ratio = scale = norm = jnp.zeros((1, 1), F32)
    for iteration in range(ITERS):
        start = iteration == 0
        if not start:
            wide_ratio = jnp.broadcast_to(ratio, vector)[None, None]
            wide_scale = jnp.broadcast_to(scale, vector)[None, None]

        def renew(x, size):
            value = residual[pl.ds(x + pad, size)]
            if start:
                return value
            slope_here = image[pl.ds(x, size)]
            if iteration > 1:
                slope_here = slope_here + wide_ratio * slope[pl.ds(x, size)]
            if iteration < ITERS - 1:
                slope[pl.ds(x, size)] = slope_here
            value = value - wide_scale * slope_here
            residual[pl.ds(x + pad, size)] = value
            return value

        def apply(i, carry):
            x = i * BLOCK
            norm_sum, image_sum, last = carry
            grown = jnp.concatenate([last, renew(x + 1, BLOCK)], 0)
            before, here, after = grown[:BLOCK], grown[1:BLOCK + 1], grown[2:]
            weight_y, weight_z = wy[pl.ds(x, BLOCK)], wz[pl.ds(x, BLOCK)]
            faces = wx[pl.ds(x, BLOCK + 1)]
            coupled = faces[1:] * after + faces[:-1] * before
            coupled = coupled + weight_y * y_after(here) + y_before(weight_y * here)
            coupled = coupled + weight_z * shift(here, -1, 3) + shift(weight_z * here, 1, 3)
            value = diag[pl.ds(x, BLOCK)] * here - coupled
            image[pl.ds(x, BLOCK)] = value
            return fold(norm_sum, here * here), fold(image_sum, here * value), grown[BLOCK:]

        opening = jnp.concatenate([jnp.zeros((1, 2, *vector), F32), renew(0, 1)], 0)
        norm_sum, image_sum, _ = lax.fori_loop(0, count // BLOCK, apply, (zero, zero, opening))
        fresh, curvature = whole(norm_sum), whole(image_sum)
        here = residual[pl.ds(first, 6)]
        if start:
            scale = fresh / curvature
            direction[...] = here
            solution[...] = jnp.broadcast_to(scale, vector)[None, None] * here
        else:
            ratio = fresh / norm
            scale = fresh / (curvature - ratio * fresh / scale)
            here = here + jnp.broadcast_to(ratio, vector)[None, None] * direction[...]
            direction[...] = here
            solution[...] = solution[...] + jnp.broadcast_to(scale, vector)[None, None] * here
        norm = fresh

    position = 2 * lax.axis_index("z") + own_core
    wanted[...] = jnp.zeros(wanted.shape, F32)
    for j in range(3):
        group = jnp.clip(position + j - 1, 0, 2 * deep - 1)
        core, row = group & 1, group >> 1
        for i in range(6):
            wanted[3 * i + j:3 * i + j + 1, :] = solution[i, core, pl.ds(row, 1), :]
    entry = lax.broadcasted_iota(jnp.int32, (BZ, 4 * BZ), 0)
    columns = lane_index((BZ, 4 * BZ))
    chosen = entry == (columns // BZ) * 32 + (columns % BZ) // 4
    spread[...] = jnp.dot(
        wanted[...], chosen.astype(F32), precision=lax.Precision.HIGHEST, preferred_element_type=F32
    )
    even = lax.axis_index("wide") % 2 == 0
    for i in range(6):
        rows = []
        for y in range(12):
            r, c = 3 * i + y // 4, y % 4
            row = spread[r:r + 1, c * BZ:(c + 1) * BZ]
            rows.append(jnp.broadcast_to(row, (2, BZ)))
        parent = jnp.concatenate(rows, 0)
        for x in (2 * i, 2 * i + 1):
            if x in (0, MX - 1):
                continue
            if x <= 2:
                value = jnp.where(even, odd_ref[x - 1], even_ref[x - 1])
            elif x >= MX - 3:
                value = jnp.where(even, even_ref[x - (MX - 3)], odd_ref[x - (MX - 3)])
            else:
                value = smooth1_ref[x]
            guess1[x] = value + active1_ref[x] * parent

    def middle_operate(ref, x):
        return operate(
            ref[x - 1], ref[x], ref[x + 1], wx1_ref[x + 1], wx1_ref[x], wy1_ref[x], wz1_ref[x],
            diag1_ref[x], active1_ref[x], 2,
        )

    def middle_first(x, slot):
        residual_here = load1_ref[x] - middle_operate(guess1, x)
        value = residual_here * (inv1_ref[x] * inverse_center)
        update1[x] = value
        second1[x] = guess1[x] + value

    loop(2, MX - 2, 4, middle_first)

    def middle_second(x, slot):
        residual_here = load1_ref[x] - middle_operate(second1, x)
        value = second1[x] + (
            carry_weight * update1[x] + fresh_weight * residual_here * inv1_ref[x]
        )
        guess1[x] = value

    loop(3, MX - 3, 3, middle_second)

    def fine_guess(x, slot):
        value = guess1[x]
        children[slot, pl.ds(0, MY, stride=2), :] = value
        children[slot, pl.ds(1, MY, stride=2), :] = value
        child = children[slot, Y0:Y0 + TY, :]
        for i in range(2):
            k = 2 * x + i - X0
            guess0[k] = smooth0_ref[k] + active0_ref[k] * child

    loop(X0 // 2, (X0 + TX) // 2, 2, fine_guess)

    def fine_operate(ref, x):
        return operate(
            ref[x - 1], ref[x], ref[x + 1], wx0_ref[x + 1], wx0_ref[x], wy0_ref[x], wz0_ref[x],
            diag0_ref[x], active0_ref[x], 1,
        )

    def fine_first(x, slot):
        residual_here = load0_ref[x] - fine_operate(guess0, x)
        value = residual_here * (inv0_ref[x] * inverse_center)
        update0[x] = value
        second0[x] = guess0[x] + value

    loop(1, TX - 1, 2, fine_first)
    margin = BX - X0

    def fine_second(x, slot):
        residual_here = load0_ref[x] - fine_operate(second0, x)
        value = second0[x] + (
            carry_weight * update0[x] + fresh_weight * residual_here * inv0_ref[x]
        )
        out_ref[x - margin] = value[BY - Y0:2 * BY - Y0]

    loop(margin, margin + BX, 2, fine_second)


def in_vmem(count):
    return [pl.BlockSpec(memory_space=pltpu.VMEM)] * count


def grids(count, *shape):
    return [jax.ShapeDtypeStruct(shape, F32)] * count


def scratch(count, *shape):
    return [pltpu.VMEM(shape, F32)] * count


def strip_part(own, before, after):
    return pl.pallas_call(
        strip_kernel,
        out_shape=grids(2, STRIP + (STRIP + 1) // 2, 8, BZ),
        in_specs=in_vmem(3),
        out_specs=in_vmem(2),
        compiler_params=pltpu.CompilerParams(vmem_limit_bytes=4 * 2**20),
        name="strip_part",
    )(own, before, after)


def local_part(own, before, after, up, down, fan):
    middle = grids(8, MX, MY, BZ)
    middle[2] = jax.ShapeDtypeStruct((MX + 1, MY, BZ), F32)
    outs = (
        grids(1, fan * ROWS, BZ) + grids(1, 2, MY, BZ) + middle + grids(8, TX, TY, BZ)
    )
    big = scratch(10, EX, EY, BZ)
    big[3] = pltpu.VMEM((EX + 1, EY, BZ), F32)
    return pl.pallas_call(
        local_kernel,
        out_shape=outs,
        in_specs=in_vmem(5),
        out_specs=in_vmem(len(outs)),
        scratch_shapes=big + scratch(2, MX, MY, BZ) + scratch(1, 2, EY, BZ)
        + scratch(1, MX, MY, BZ) + scratch(1, MY, BZ),
        compiler_params=pltpu.CompilerParams(vmem_limit_bytes=24 * 2**20),
        name="local_part",
    )(own, before, after, up, down)


def finish_part(wide, deep, mine, other, even, odd, kept):
    count = 2 * wide
    tile = (2, deep, BZ)
    return pl.pallas_call(
        functools.partial(finish_kernel, wide, deep),
        out_shape=jax.ShapeDtypeStruct((BX, BY, BZ), F32),
        in_specs=in_vmem(4 + len(kept)),
        out_specs=pl.BlockSpec(memory_space=pltpu.VMEM),
        scratch_shapes=scratch(3, count + 1, *tile)
        + scratch(3, count, *tile) + scratch(1, count + 4, *tile) + scratch(2, count + 1, *tile)
        + scratch(2, 6, *tile) + scratch(1, 24, BZ) + scratch(1, 24, 4 * BZ)
        + scratch(3, MX, MY, BZ) + scratch(1, 2, EY, BZ) + scratch(3, TX, TY, BZ),
        compiler_params=pltpu.CompilerParams(vmem_limit_bytes=24 * 2**20),
        name="finish_part",
    )(mine, other, even, odd, *kept)


def upward(size):
    return [(i, i + 1) for i in range(size - 1)]


def downward(size):
    return [(i + 1, i) for i in range(size - 1)]


def swapped(size, start):
    pairs = [(i, i + 1) for i in range(start, size - 1, 2)]
    return pairs + [(j, i) for i, j in pairs]


def pack_kernel(
    source_ref, coef_ref, tops_ref, own_ref, right_ref, left_ref, tops, sems
):
    moves = (
        (tops_ref, tops),
        (source_ref, own_ref.at[pl.ds(0, BX)]),
        (coef_ref, own_ref.at[pl.ds(BX, BX)]),
        (source_ref.at[pl.ds(BX - NS, NS)], right_ref.at[pl.ds(0, NS)]),
        (coef_ref.at[pl.ds(BX - NC, NC)], right_ref.at[pl.ds(NS, NC)]),
        (source_ref.at[pl.ds(0, NS)], left_ref.at[pl.ds(0, NS)]),
        (coef_ref.at[pl.ds(0, NC)], left_ref.at[pl.ds(NS, NC)]),
    )
    copies = [pltpu.make_async_copy(*move, sems.at[i]) for i, move in enumerate(moves)]
    for copy in copies:
        copy.start()
    copies[0].wait()
    values = tops[...].astype(F32)
    same = lax.broadcasted_iota(jnp.int32, (BY, BY), 0) == lane_index((BY, BY))
    lanes = lane_index((BY, BZ))
    turned = jnp.zeros((BY, BZ), F32)
    for x in range(BX):
        column = jnp.sum(jnp.where(same, values[x:x + 1], 0.0), axis=1, keepdims=True)
        turned = jnp.where(lanes == x, column, turned)
    own_ref[PACK - 1] = turned
    right_ref[SIDE - 1] = turned
    left_ref[SIDE - 1] = turned
    for copy in copies[1:]:
        copy.wait()


def pack_part(source, conductivity, ice_cells):
    return pl.pallas_call(
        pack_kernel,
        out_shape=grids(1, PACK, BY, BZ) + grids(2, SIDE, BY, BZ),
        in_specs=[pl.BlockSpec(memory_space=pltpu.HBM)] * 3,
        out_specs=in_vmem(3),
        scratch_shapes=[pltpu.VMEM((BX, BY), jnp.int32), pltpu.SemaphoreType.DMA((7,))],
        compiler_params=pltpu.CompilerParams(vmem_limit_bytes=4 * 2**20),
        name="pack_part",
    )(source, conductivity, ice_cells)


def shards(wide, deep, source, conductivity, ice_cells):
    own, right, left = pack_part(source, conductivity, ice_cells)
    before = lax.ppermute(right, "wide", upward(wide))
    after = lax.ppermute(left, "wide", downward(wide))
    up, down = strip_part(own, before, after)
    up = lax.ppermute(up, ("z", "core"), upward(2 * deep))
    down = lax.ppermute(down, ("z", "core"), downward(2 * deep))
    fan, edge, *kept = local_part(own, before, after, up, down, wide * deep)
    even = lax.ppermute(edge, "wide", swapped(wide, 0))
    odd = lax.ppermute(edge, "wide", swapped(wide, 1))
    fan = fan.reshape(wide * deep, 1, ROWS * BZ)
    mine = lax.all_to_all(fan, ("wide", "z"), 0, 0, tiled=True)
    mine = mine.reshape(wide * deep * ROWS, BZ)
    other = lax.ppermute(mine, "core", [(0, 1), (1, 0)])
    return finish_part(wide, deep, mine, other, even, odd, kept)


def solution(mesh):
    wide, deep = mesh.shape["wide"], mesh.shape["grp"] // 2
    split = Mesh(mesh.devices.reshape(wide, deep, 2), ("wide", "z", "core"))
    group = ("z", "core")
    return jax.shard_map(
        functools.partial(shards, wide, deep),
        mesh=split,
        in_specs=(P("wide", group, None), P("wide", group, None), P("wide", group)),
        out_specs=P("wide", group, None),
        check_vma=False,
    )
```

profile of v0, /device:TPU:8, one launch (start us, length us, event | category | flops | bytes accessed | tf_op | source)
XLA Modules:
  0.0 98.0 jit_solution(11226329832292837352)
XLA Ops:
  0.0 0.0 copy-start
  0.0 0.8 copy-done
  0.8 0.0 copy-start.1
  0.8 0.8 copy-done.1
  1.7 0.0 copy-start.2
  1.7 0.7 copy-done.2
  2.4 0.6 pack_part.1
  3.0 3.5 %collective-permute-start = (f32[14,16,128]{2,1,0:T(8,128)S(1)}, f32[14,16,128]{2,1,0:T(8,128)S(1)}, u32[]{:S(2)}, u32[]{:S(2)}) collective-permute-start(f32[14,16,128]{2,1,0:T(8,128)S(1)} %get-tuple-element.29), channel_id=1, source_target_pairs={{0,16},{16,32},{32,48},{48,64},{64,80},{80,96},{96,112},{112,128},... | collective-permute-start | bytes 344072 | tf_op jit(solution)/shard_map/ppermute | solution.py:654
  6.5 5.5 %collective-permute-start.1 = (f32[14,16,128]{2,1,0:T(8,128)S(1)}, f32[14,16,128]{2,1,0:T(8,128)S(1)}, u32[]{:S(2)}, u32[]{:S(2)}) collective-permute-start(f32[14,16,128]{2,1,0:T(8,128)S(1)} %get-tuple-element.30), channel_id=1, source_target_pairs={{16,0},{32,16},{48,32},{64,48},{80,64},{96,80},{112,96},{128,112},... | collective-permute-start | bytes 344072 | tf_op jit(solution)/shard_map/ppermute | solution.py:655
  12.0 0.8 collective-permute-done.before_ref
  12.8 1.5 %collective-permute-done.1.after_ref = f32[14,16,128]{2,1,0:T(8,128)S(1)} collective-permute-done((f32[14,16,128]{2,1,0:T(8,128)S(1)}, f32[14,16,128]{2,1,0:T(8,128)S(1)}, u32[]{:S(2)}, u32[]{:S(2)}) %collective-permute-start.1) | collective-permute-done | bytes 114720 | tf_op jit(solution)/shard_map/ppermute | solution.py:655
  14.4 1.3 %collective-permute-start.2 = (f32[68,8,128]{2,1,0:T(8,128)S(1)}, f32[68,8,128]{2,1,0:T(8,128)S(1)}, u32[]{:S(2)}, u32[]{:S(2)}) collective-permute-start(f32[68,8,128]{2,1,0:T(8,128)S(1)} %get-tuple-element.31), channel_id=1, source_target_pairs={{0,1},{1,2},{2,3},{3,4},{4,5},{5,6},{6,7},{7,8},{8,9},{9,10},{10,1... | collective-permute-start | bytes 835592 | tf_op jit(solution)/shard_map/ppermute | solution.py:657
  15.7 1.3 %collective-permute-start.3 = (f32[68,8,128]{2,1,0:T(8,128)S(1)}, f32[68,8,128]{2,1,0:T(8,128)S(1)}, u32[]{:S(2)}, u32[]{:S(2)}) collective-permute-start(f32[68,8,128]{2,1,0:T(8,128)S(1)} %get-tuple-element.32), channel_id=1, source_target_pairs={{1,0},{2,1},{3,2},{4,3},{5,4},{6,5},{7,6},{8,7},{9,8},{10,9},{11,1... | collective-permute-start | bytes 835592 | tf_op jit(solution)/shard_map/ppermute | solution.py:658
  17.0 0.0 collective-permute-done.2.up_ref
  17.0 3.6 %collective-permute-done.3.down_ref = f32[68,8,128]{2,1,0:T(8,128)S(1)} collective-permute-done((f32[68,8,128]{2,1,0:T(8,128)S(1)}, f32[68,8,128]{2,1,0:T(8,128)S(1)}, u32[]{:S(2)}, u32[]{:S(2)}) %collective-permute-start.3) | collective-permute-done | bytes 278560 | tf_op jit(solution)/shard_map/ppermute | solution.py:658
  20.6 6.0 %local_part.1 = (f32[1280,128]{1,0:T(8,128)S(1)}, f32[2,24,128]{2,1,0:T(8,128)S(1)}, f32[12,24,128]{2,1,0:T(8,128)S(1)}, f32[12,24,128]{2,1,0:T(8,128)S(1)}, f32...) custom-call(f32[17,16,128]{2,1,0:T(8,128)S(1)} %get-tuple-element.28, ...), custom_call_target="tpu_custom_call" | custom-call | tf_op jit(solution)/shard_map/local_part/pallas_call | solution.py:568
  26.6 50.6 %all_to_all.5 = f32[256,1,640]{2,1,0:T(1,128)S(1)} all-to-all(f32[256,1,640]{2,1,0:T(1,128)S(1)} %bitcast.4), channel_id=1, replica_groups=mesh['wide'=32,'z'=8,'core'=2] {'wide','z'}, dimensions={0} | all-to-all | bytes 1310720 | tf_op jit(solution)/shard_map/all_to_all | solution.py:663
  77.2 1.9 %collective-permute-start.4 = (f32[1280,128]{1,0:T(8,128)S(1)}, f32[1280,128]{1,0:T(8,128)S(1)}, u32[]{:S(2)}, u32[]{:S(2)}) collective-permute-start(f32[1280,128]{1,0:T(8,128)S(1)} %bitcast.2), channel_id=1, source_target_pairs={{0,1},{1,0},{2,3},{3,2},{4,5},{5,4},{6,7},{7,6},{8,9},{9,8},{10,11... | collective-permute-start | bytes 1966088 | tf_op jit(solution)/shard_map/ppermute | solution.py:665
  79.1 2.6 %collective-permute-start.6 = (f32[2,24,128]{2,1,0:T(8,128)S(1)}, f32[2,24,128]{2,1,0:T(8,128)S(1)}, u32[]{:S(2)}, u32[]{:S(2)}) collective-permute-start(f32[2,24,128]{2,1,0:T(8,128)S(1)} %get-tuple-element.34), channel_id=1, source_target_pairs={{16,32},{48,64},{80,96},{112,128},{144,160},{176,192},{208,224},{2... | collective-permute-start | bytes 73736 | tf_op jit(solution)/shard_map/ppermute | solution.py:661
  81.7 1.9 %collective-permute-start.5 = (f32[2,24,128]{2,1,0:T(8,128)S(1)}, f32[2,24,128]{2,1,0:T(8,128)S(1)}, u32[]{:S(2)}, u32[]{:S(2)}) collective-permute-start(f32[2,24,128]{2,1,0:T(8,128)S(1)} %get-tuple-element.34), channel_id=1, source_target_pairs={{0,16},{32,48},{64,80},{96,112},{128,144},{160,176},{192,208},{224... | collective-permute-start | bytes 73736 | tf_op jit(solution)/shard_map/ppermute | solution.py:660
  83.7 1.2 %collective-permute-done.6.odd_ref = f32[2,24,128]{2,1,0:T(8,128)S(1)} collective-permute-done((f32[2,24,128]{2,1,0:T(8,128)S(1)}, f32[2,24,128]{2,1,0:T(8,128)S(1)}, u32[]{:S(2)}, u32[]{:S(2)}) %collective-permute-start.6) | collective-permute-done | bytes 24608 | tf_op jit(solution)/shard_map/ppermute | solution.py:661
  84.9 2.6 %collective-permute-done.5.even_ref = f32[2,24,128]{2,1,0:T(8,128)S(1)} collective-permute-done((f32[2,24,128]{2,1,0:T(8,128)S(1)}, f32[2,24,128]{2,1,0:T(8,128)S(1)}, u32[]{:S(2)}, u32[]{:S(2)}) %collective-permute-start.5) | collective-permute-done | bytes 24608 | tf_op jit(solution)/shard_map/ppermute | solution.py:660
  87.5 0.0 collective-permute-done.4.other_ref
  87.5 10.5 %finish_part.1 = f32[8,16,128]{2,1,0:T(8,128)} custom-call(f32[1280,128]{1,0:T(8,128)S(1)} %bitcast.3, f32[1280,128]{1,0:T(8,128)S(1)} %collective-permute-done.4.other_ref, f32[2,24,128]{2,1,0:T(8,128)S(1)} %collective-permute-done.5.even_ref, f32[2,24,128]{2,1,0:T(8,128)S(1)} %collective-permute-done.6.odd_ref, ...), custom_call_target="tpu_custom_call" | custom-call | tf_op jit(solution)/shard_map/finish_part/pallas_call | solution.py:583
  (1 shorter events, 0.0 us)
Async XLA Ops:
  0.0 0.8 copy-start
  0.8 0.8 copy-start.1
  1.7 0.7 copy-start.2
  3.0 9.8 %collective-permute-start = (f32[14,16,128]{2,1,0:T(8,128)S(1)}, f32[14,16,128]{2,1,0:T(8,128)S(1)}, u32[]{:S(2)}, u32[]{:S(2)}) collective-permute-start(f32[14,16,128]{2,1,0:T(8,128)S(1)} %get-tuple-element.29), channel_id=1, source_target_pairs={{0,16},{16,32},{32,48},{48,64},{64,80},{80,96},{96,112},{112,128},... | collective-permute-start | bytes 344072 | tf_op jit(solution)/shard_map/ppermute | solution.py:654
  6.5 7.9 %collective-permute-start.1 = (f32[14,16,128]{2,1,0:T(8,128)S(1)}, f32[14,16,128]{2,1,0:T(8,128)S(1)}, u32[]{:S(2)}, u32[]{:S(2)}) collective-permute-start(f32[14,16,128]{2,1,0:T(8,128)S(1)} %get-tuple-element.30), channel_id=1, source_target_pairs={{16,0},{32,16},{48,32},{64,48},{80,64},{96,80},{112,96},{128,112},... | collective-permute-start | bytes 344072 | tf_op jit(solution)/shard_map/ppermute | solution.py:655
  14.4 2.6 %collective-permute-start.2 = (f32[68,8,128]{2,1,0:T(8,128)S(1)}, f32[68,8,128]{2,1,0:T(8,128)S(1)}, u32[]{:S(2)}, u32[]{:S(2)}) collective-permute-start(f32[68,8,128]{2,1,0:T(8,128)S(1)} %get-tuple-element.31), channel_id=1, source_target_pairs={{0,1},{1,2},{2,3},{3,4},{4,5},{5,6},{6,7},{7,8},{8,9},{9,10},{10,1... | collective-permute-start | bytes 835592 | tf_op jit(solution)/shard_map/ppermute | solution.py:657
  15.7 4.9 %collective-permute-start.3 = (f32[68,8,128]{2,1,0:T(8,128)S(1)}, f32[68,8,128]{2,1,0:T(8,128)S(1)}, u32[]{:S(2)}, u32[]{:S(2)}) collective-permute-start(f32[68,8,128]{2,1,0:T(8,128)S(1)} %get-tuple-element.32), channel_id=1, source_target_pairs={{1,0},{2,1},{3,2},{4,3},{5,4},{6,5},{7,6},{8,7},{9,8},{10,9},{11,1... | collective-permute-start | bytes 835592 | tf_op jit(solution)/shard_map/ppermute | solution.py:658
  77.2 10.3 %collective-permute-start.4 = (f32[1280,128]{1,0:T(8,128)S(1)}, f32[1280,128]{1,0:T(8,128)S(1)}, u32[]{:S(2)}, u32[]{:S(2)}) collective-permute-start(f32[1280,128]{1,0:T(8,128)S(1)} %bitcast.2), channel_id=1, source_target_pairs={{0,1},{1,0},{2,3},{3,2},{4,5},{5,4},{6,7},{7,6},{8,9},{9,8},{10,11... | collective-permute-start | bytes 1966088 | tf_op jit(solution)/shard_map/ppermute | solution.py:665
  79.1 5.7 %collective-permute-start.6 = (f32[2,24,128]{2,1,0:T(8,128)S(1)}, f32[2,24,128]{2,1,0:T(8,128)S(1)}, u32[]{:S(2)}, u32[]{:S(2)}) collective-permute-start(f32[2,24,128]{2,1,0:T(8,128)S(1)} %get-tuple-element.34), channel_id=1, source_target_pairs={{16,32},{48,64},{80,96},{112,128},{144,160},{176,192},{208,224},{2... | collective-permute-start | bytes 73736 | tf_op jit(solution)/shard_map/ppermute | solution.py:661
  81.7 5.7 %collective-permute-start.5 = (f32[2,24,128]{2,1,0:T(8,128)S(1)}, f32[2,24,128]{2,1,0:T(8,128)S(1)}, u32[]{:S(2)}, u32[]{:S(2)}) collective-permute-start(f32[2,24,128]{2,1,0:T(8,128)S(1)} %get-tuple-element.34), channel_id=1, source_target_pairs={{0,16},{32,48},{64,80},{96,112},{128,144},{160,176},{192,208},{224... | collective-permute-start | bytes 73736 | tf_op jit(solution)/shard_map/ppermute | solution.py:660
where the time goes:
time: 98.4 us; the launch traced here: 98 us
  blocking collectives  50.6 us (51%)
  starting transfers between devices  18 us (18%)
  Pallas kernels  17.2 us (17%)
  waiting for transfers between devices  9.69 us (10%)
  local copies, waits for them, and re-layouts  2.36 us (2%)
    all_to_all x1, blocking collectives, shards(): mine = lax.all_to_all(fan, ('wide', 'z'), 0, 0, tiled=True)  50.6 us
    pallas_call x1, Pallas kernels, finish_part(): pl.pallas_call(functools.partial(finish_kernel, wide, deep), out_shape=ja...  10.5 us
    pallas_call x1, Pallas kernels, local_part(): pl.pallas_call(local_kernel, out_shape=outs, in_specs=in_vmem(5), out_spe...  6.02 us
    ppermute x1, starting transfers between devices, shards(): after = lax.ppermute(left, 'wide', downward(wide))  5.51 us
    ppermute x1, waiting for transfers between devices, shards(): down = lax.ppermute(down, ('z', 'core'), downward(2 * deep))  3.55 us
    ppermute x1, starting transfers between devices, shards(): before = lax.ppermute(right, 'wide', upward(wide))  3.48 us
    ppermute x1, waiting for transfers between devices, shards(): even = lax.ppermute(edge, 'wide', swapped(wide, 0))  2.61 us
    ppermute x1, starting transfers between devices, shards(): odd = lax.ppermute(edge, 'wide', swapped(wide, 1))  2.6 us
  transfers between devices with their start and end apart: 7, of which 5 were waited for; matrix products, arithmetic and copies ran while one was open for 0% of the time, Pallas kernels for 0%

commit v1 on v0

--- a/solution.py
+++ b/solution.py
@@ -287,13 +287,9 @@
     lax.fori_loop(0, fan_ref.shape[0] // (8 * ROWS), fan, 0)
 
 
-def finish_kernel(
-    wide, deep, mine_ref, other_ref, even_ref, odd_ref,
-    load1_ref, active1_ref, wx1_ref, wy1_ref, wz1_ref, diag1_ref, inv1_ref, smooth1_ref,
-    load0_ref, active0_ref, wx0_ref, wy0_ref, wz0_ref, diag0_ref, inv0_ref, smooth0_ref,
-    out_ref,
-    coef, active, wx, wy, wz, diag, residual, image, slope, direction, solution, wanted, spread,
-    guess1, update1, second1, children, guess0, update0, second0,
+def coarse_kernel(
+    wide, deep, mine_ref, other_ref, wanted,
+    coef, active, wx, wy, wz, diag, residual, image, slope, direction, solution,
 ):
     count = 2 * wide
     vector = (deep, BZ)
@@ -450,6 +446,15 @@
         core, row = group & 1, group >> 1
         for i in range(6):
             wanted[3 * i + j:3 * i + j + 1, :] = solution[i, core, pl.ds(row, 1), :]
+
+
+def finish_kernel(
+    wanted, even_ref, odd_ref,
+    load1_ref, active1_ref, wx1_ref, wy1_ref, wz1_ref, diag1_ref, inv1_ref, smooth1_ref,
+    load0_ref, active0_ref, wx0_ref, wy0_ref, wz0_ref, diag0_ref, inv0_ref, smooth0_ref,
+    out_ref,
+    spread, guess1, update1, second1, children, guess0, update0, second0,
+):
     entry = lax.broadcasted_iota(jnp.int32, (BZ, 4 * BZ), 0)
     columns = lane_index((BZ, 4 * BZ))
     chosen = entry == (columns // BZ) * 32 + (columns % BZ) // 4
@@ -577,21 +582,35 @@
     )(own, before, after, up, down)
 
 
-def finish_part(wide, deep, mine, other, even, odd, kept):
+def coarse_part(wide, deep, mine, other):
     count = 2 * wide
     tile = (2, deep, BZ)
+    work = count * 2 * deep * BZ
     return pl.pallas_call(
-        functools.partial(finish_kernel, wide, deep),
-        out_shape=jax.ShapeDtypeStruct((BX, BY, BZ), F32),
-        in_specs=in_vmem(4 + len(kept)),
+        functools.partial(coarse_kernel, wide, deep),
+        out_shape=jax.ShapeDtypeStruct((24, BZ), F32),
+        in_specs=in_vmem(2),
         out_specs=pl.BlockSpec(memory_space=pltpu.VMEM),
         scratch_shapes=scratch(3, count + 1, *tile)
         + scratch(3, count, *tile) + scratch(1, count + 4, *tile) + scratch(2, count + 1, *tile)
-        + scratch(2, 6, *tile) + scratch(1, 24, BZ) + scratch(1, 24, 4 * BZ)
+        + scratch(2, 6, *tile),
+        compiler_params=pltpu.CompilerParams(vmem_limit_bytes=16 * 2**20),
+        cost_estimate=pl.CostEstimate(flops=250 * work, bytes_accessed=8 * work * 4, transcendentals=0),
+        name="coarse_part",
+    )(mine, other)
+
+
+def finish_part(wanted, even, odd, kept):
+    return pl.pallas_call(
+        finish_kernel,
+        out_shape=jax.ShapeDtypeStruct((BX, BY, BZ), F32),
+        in_specs=in_vmem(3 + len(kept)),
+        out_specs=pl.BlockSpec(memory_space=pltpu.VMEM),
+        scratch_shapes=scratch(1, 24, 4 * BZ)
         + scratch(3, MX, MY, BZ) + scratch(1, 2, EY, BZ) + scratch(3, TX, TY, BZ),
-        compiler_params=pltpu.CompilerParams(vmem_limit_bytes=24 * 2**20),
+        compiler_params=pltpu.CompilerParams(vmem_limit_bytes=8 * 2**20),
         name="finish_part",
-    )(mine, other, even, odd, *kept)
+    )(wanted, even, odd, *kept)
 
 
 def upward(size):
@@ -646,7 +665,7 @@
         scratch_shapes=[pltpu.VMEM((BX, BY), jnp.int32), pltpu.SemaphoreType.DMA((7,))],
         compiler_params=pltpu.CompilerParams(vmem_limit_bytes=4 * 2**20),
         name="pack_part",
-    )(source, conductivity, ice_cells)
+    )(*(pltpu.with_memory_space_constraint(v, pltpu.HBM) for v in (source, conductivity, ice_cells)))
 
 
 def shards(wide, deep, source, conductivity, ice_cells):
@@ -657,13 +676,14 @@
     up = lax.ppermute(up, ("z", "core"), upward(2 * deep))
     down = lax.ppermute(down, ("z", "core"), downward(2 * deep))
     fan, edge, *kept = local_part(own, before, after, up, down, wide * deep)
-    even = lax.ppermute(edge, "wide", swapped(wide, 0))
-    odd = lax.ppermute(edge, "wide", swapped(wide, 1))
     fan = fan.reshape(wide * deep, 1, ROWS * BZ)
     mine = lax.all_to_all(fan, ("wide", "z"), 0, 0, tiled=True)
     mine = mine.reshape(wide * deep * ROWS, BZ)
     other = lax.ppermute(mine, "core", [(0, 1), (1, 0)])
-    return finish_part(wide, deep, mine, other, even, odd, kept)
+    even = lax.ppermute(edge, "wide", swapped(wide, 0))
+    odd = lax.ppermute(edge, "wide", swapped(wide, 1))
+    wanted = coarse_part(wide, deep, mine, other)
+    return finish_part(wanted, even, odd, kept)
 
 
 def solution(mesh):

time: 98.4 us -> 95.2 us (0.967)
  the two profiles are of different devices: /device:TPU:8 before, /device:TPU:1 now
where the time goes in v1:
time: 95.2 us; the launch traced here: 94.9 us
  blocking collectives  44 us (46%)
  starting transfers between devices  23.4 us (25%)
  Pallas kernels  17.7 us (19%)
  waiting for transfers between devices  9.62 us (10%)
    all_to_all x1, blocking collectives, shards(): mine = lax.all_to_all(fan, ('wide', 'z'), 0, 0, tiled=True)  44 us
    pallas_call x1, Pallas kernels, coarse_part(): pl.pallas_call(functools.partial(coarse_kernel, wide, deep), out_shape=ja...  8.39 us
    pallas_call x1, Pallas kernels, local_part(): pl.pallas_call(local_kernel, out_shape=outs, in_specs=in_vmem(5), out_spe...  6.03 us
    ppermute x1, starting transfers between devices, shards(): up = lax.ppermute(up, ('z', 'core'), upward(2 * deep))  5.99 us
    ppermute x1, starting transfers between devices, shards(): even = lax.ppermute(edge, 'wide', swapped(wide, 0))  5.83 us
    ppermute x1, waiting for transfers between devices, shards(): down = lax.ppermute(down, ('z', 'core'), downward(2 * deep))  4.4 us
    ppermute x1, starting transfers between devices, shards(): before = lax.ppermute(right, 'wide', upward(wide))  4.02 us
    ppermute x1, waiting for transfers between devices, shards(): after = lax.ppermute(left, 'wide', downward(wide))  3.7 us
  transfers between devices with their start and end apart: 7, of which 4 were waited for; matrix products, arithmetic and copies ran while one was open for 0% of the time, Pallas kernels for 9%

profile of v1, /device:TPU:1, one launch (start us, length us, event | category | flops | bytes accessed | tf_op | source)
XLA Modules:
  0.0 94.9 jit_solution(13371342976073538534)
XLA Ops:
  0.0 1.0 %pack_part.1 = (f32[17,16,128]{2,1,0:T(8,128)S(1)}, f32[14,16,128]{2,1,0:T(8,128)S(1)}, f32[14,16,128]{2,1,0:T(8,128)S(1)}) custom-call(f32[8,16,128]{2,1,0:T(8,128)} %source_ref.1, f32[8,16,128]{2,1,0:T(8,128)} %coef_ref.1, s32[8,16]{1,0:T(8,128)} %tops_ref.1), custom_call_target="tpu_custom_call" | custom-call | tf_op jit(solution)/shard_map/pack_part/pallas_call | solution.py:660
  1.0 4.0 %collective-permute-start = (f32[14,16,128]{2,1,0:T(8,128)S(1)}, f32[14,16,128]{2,1,0:T(8,128)S(1)}, u32[]{:S(2)}, u32[]{:S(2)}) collective-permute-start(f32[14,16,128]{2,1,0:T(8,128)S(1)} %get-tuple-element.29), channel_id=1, source_target_pairs={{0,16},{16,32},{32,48},{48,64},{64,80},{80,96},{96,112},{112,128},... | collective-permute-start | bytes 344072 | tf_op jit(solution)/shard_map/ppermute | solution.py:673
  5.1 1.3 %collective-permute-start.1 = (f32[14,16,128]{2,1,0:T(8,128)S(1)}, f32[14,16,128]{2,1,0:T(8,128)S(1)}, u32[]{:S(2)}, u32[]{:S(2)}) collective-permute-start(f32[14,16,128]{2,1,0:T(8,128)S(1)} %get-tuple-element.30), channel_id=1, source_target_pairs={{16,0},{32,16},{48,32},{64,48},{80,64},{96,80},{112,96},{128,112},... | collective-permute-start | bytes 344072 | tf_op jit(solution)/shard_map/ppermute | solution.py:674
  6.4 0.5 collective-permute-done.before_ref
  6.9 3.7 %collective-permute-done.1.after_ref = f32[14,16,128]{2,1,0:T(8,128)S(1)} collective-permute-done((f32[14,16,128]{2,1,0:T(8,128)S(1)}, f32[14,16,128]{2,1,0:T(8,128)S(1)}, u32[]{:S(2)}, u32[]{:S(2)}) %collective-permute-start.1) | collective-permute-done | bytes 114720 | tf_op jit(solution)/shard_map/ppermute | solution.py:674
  10.7 6.0 %collective-permute-start.2 = (f32[68,8,128]{2,1,0:T(8,128)S(1)}, f32[68,8,128]{2,1,0:T(8,128)S(1)}, u32[]{:S(2)}, u32[]{:S(2)}) collective-permute-start(f32[68,8,128]{2,1,0:T(8,128)S(1)} %get-tuple-element.31), channel_id=1, source_target_pairs={{0,1},{1,2},{2,3},{3,4},{4,5},{5,6},{6,7},{7,8},{8,9},{9,10},{10,1... | collective-permute-start | bytes 835592 | tf_op jit(solution)/shard_map/ppermute | solution.py:676
  16.7 2.5 %collective-permute-start.3 = (f32[68,8,128]{2,1,0:T(8,128)S(1)}, f32[68,8,128]{2,1,0:T(8,128)S(1)}, u32[]{:S(2)}, u32[]{:S(2)}) collective-permute-start(f32[68,8,128]{2,1,0:T(8,128)S(1)} %get-tuple-element.32), channel_id=1, source_target_pairs={{1,0},{2,1},{3,2},{4,3},{5,4},{6,5},{7,6},{8,7},{9,8},{10,9},{11,1... | collective-permute-start | bytes 835592 | tf_op jit(solution)/shard_map/ppermute | solution.py:677
  19.2 1.0 %collective-permute-done.2.up_ref = f32[68,8,128]{2,1,0:T(8,128)S(1)} collective-permute-done((f32[68,8,128]{2,1,0:T(8,128)S(1)}, f32[68,8,128]{2,1,0:T(8,128)S(1)}, u32[]{:S(2)}, u32[]{:S(2)}) %collective-permute-start.2) | collective-permute-done | bytes 278560 | tf_op jit(solution)/shard_map/ppermute | solution.py:676
  20.1 4.4 %collective-permute-done.3.down_ref = f32[68,8,128]{2,1,0:T(8,128)S(1)} collective-permute-done((f32[68,8,128]{2,1,0:T(8,128)S(1)}, f32[68,8,128]{2,1,0:T(8,128)S(1)}, u32[]{:S(2)}, u32[]{:S(2)}) %collective-permute-start.3) | collective-permute-done | bytes 278560 | tf_op jit(solution)/shard_map/ppermute | solution.py:677
  24.5 6.0 %local_part.1 = (f32[1280,128]{1,0:T(8,128)S(1)}, f32[2,24,128]{2,1,0:T(8,128)S(1)}, f32[12,24,128]{2,1,0:T(8,128)S(1)}, f32[12,24,128]{2,1,0:T(8,128)S(1)}, f32...) custom-call(f32[17,16,128]{2,1,0:T(8,128)S(1)} %get-tuple-element.28, ...), custom_call_target="tpu_custom_call" | custom-call | tf_op jit(solution)/shard_map/local_part/pallas_call | solution.py:573
  30.6 44.0 %all_to_all.5 = f32[256,1,640]{2,1,0:T(1,128)S(1)} all-to-all(f32[256,1,640]{2,1,0:T(1,128)S(1)} %bitcast.4), channel_id=1, replica_groups=mesh['wide'=32,'z'=8,'core'=2] {'wide','z'}, dimensions={0} | all-to-all | bytes 1310720 | tf_op jit(solution)/shard_map/all_to_all | solution.py:680
  74.6 3.1 %collective-permute-start.4 = (f32[1280,128]{1,0:T(8,128)S(1)}, f32[1280,128]{1,0:T(8,128)S(1)}, u32[]{:S(2)}, u32[]{:S(2)}) collective-permute-start(f32[1280,128]{1,0:T(8,128)S(1)} %bitcast.2), channel_id=1, source_target_pairs={{0,1},{1,0},{2,3},{3,2},{4,5},{5,4},{6,7},{7,6},{8,9},{9,8},{10,11... | collective-permute-start | bytes 1966088 | tf_op jit(solution)/shard_map/ppermute | solution.py:682
  77.7 0.7 collective-permute-start.6
  78.4 5.8 %collective-permute-start.5 = (f32[2,24,128]{2,1,0:T(8,128)S(1)}, f32[2,24,128]{2,1,0:T(8,128)S(1)}, u32[]{:S(2)}, u32[]{:S(2)}) collective-permute-start(f32[2,24,128]{2,1,0:T(8,128)S(1)} %get-tuple-element.34), channel_id=1, source_target_pairs={{0,16},{32,48},{64,80},{96,112},{128,144},{160,176},{192,208},{224... | collective-permute-start | bytes 73736 | tf_op jit(solution)/shard_map/ppermute | solution.py:683
  84.2 0.0 collective-permute-done.4.other_ref
  84.2 8.4 %coarse_part.1.wanted = f32[24,128]{1,0:T(8,128)S(1)} custom-call(f32[1280,128]{1,0:T(8,128)S(1)} %bitcast.3, f32[1280,128]{1,0:T(8,128)S(1)} %collective-permute-done.4.other_ref), custom_call_target="tpu_custom_call" | custom-call | flops 32768000 | bytes 4194304 | tf_op jit(solution)/shard_map/coarse_part/pallas_call | solution.py:589
  92.6 0.0 collective-permute-done.6.odd_ref
  92.7 0.0 collective-permute-done.5.even_ref
  92.7 2.2 %finish_part.1 = f32[8,16,128]{2,1,0:T(8,128)} custom-call(f32[24,128]{1,0:T(8,128)S(1)} %coarse_part.1.wanted, f32[2,24,128]{2,1,0:T(8,128)S(1)} %collective-permute-done.5.even_ref, f32[2,24,128]{2,1,0:T(8,128)S(1)} %collective-permute-done.6.odd_ref, f32[12,24,128]{2,1,0:T(8,128)S(1)} %get-tuple-element.35.load1_ref, ...), custom_call_target="tpu_custom_call" | custom-call | tf_op jit(solution)/shard_map/finish_part/pallas_call | solution.py:604
  (1 shorter events, 0.0 us)
Async XLA Ops:
  1.0 5.9 %collective-permute-start = (f32[14,16,128]{2,1,0:T(8,128)S(1)}, f32[14,16,128]{2,1,0:T(8,128)S(1)}, u32[]{:S(2)}, u32[]{:S(2)}) collective-permute-start(f32[14,16,128]{2,1,0:T(8,128)S(1)} %get-tuple-element.29), channel_id=1, source_target_pairs={{0,16},{16,32},{32,48},{48,64},{64,80},{80,96},{96,112},{112,128},... | collective-permute-start | bytes 344072 | tf_op jit(solution)/shard_map/ppermute | solution.py:673
  5.1 5.5 %collective-permute-start.1 = (f32[14,16,128]{2,1,0:T(8,128)S(1)}, f32[14,16,128]{2,1,0:T(8,128)S(1)}, u32[]{:S(2)}, u32[]{:S(2)}) collective-permute-start(f32[14,16,128]{2,1,0:T(8,128)S(1)} %get-tuple-element.30), channel_id=1, source_target_pairs={{16,0},{32,16},{48,32},{64,48},{80,64},{96,80},{112,96},{128,112},... | collective-permute-start | bytes 344072 | tf_op jit(solution)/shard_map/ppermute | solution.py:674
  10.7 9.5 %collective-permute-start.2 = (f32[68,8,128]{2,1,0:T(8,128)S(1)}, f32[68,8,128]{2,1,0:T(8,128)S(1)}, u32[]{:S(2)}, u32[]{:S(2)}) collective-permute-start(f32[68,8,128]{2,1,0:T(8,128)S(1)} %get-tuple-element.31), channel_id=1, source_target_pairs={{0,1},{1,2},{2,3},{3,4},{4,5},{5,6},{6,7},{7,8},{8,9},{9,10},{10,1... | collective-permute-start | bytes 835592 | tf_op jit(solution)/shard_map/ppermute | solution.py:676
  16.7 7.9 %collective-permute-start.3 = (f32[68,8,128]{2,1,0:T(8,128)S(1)}, f32[68,8,128]{2,1,0:T(8,128)S(1)}, u32[]{:S(2)}, u32[]{:S(2)}) collective-permute-start(f32[68,8,128]{2,1,0:T(8,128)S(1)} %get-tuple-element.32), channel_id=1, source_target_pairs={{1,0},{2,1},{3,2},{4,3},{5,4},{6,5},{7,6},{8,7},{9,8},{10,9},{11,1... | collective-permute-start | bytes 835592 | tf_op jit(solution)/shard_map/ppermute | solution.py:677
  74.6 9.6 %collective-permute-start.4 = (f32[1280,128]{1,0:T(8,128)S(1)}, f32[1280,128]{1,0:T(8,128)S(1)}, u32[]{:S(2)}, u32[]{:S(2)}) collective-permute-start(f32[1280,128]{1,0:T(8,128)S(1)} %bitcast.2), channel_id=1, source_target_pairs={{0,1},{1,0},{2,3},{3,2},{4,5},{5,4},{6,7},{7,6},{8,9},{9,8},{10,11... | collective-permute-start | bytes 1966088 | tf_op jit(solution)/shard_map/ppermute | solution.py:682
  77.7 14.9 %collective-permute-start.6 = (f32[2,24,128]{2,1,0:T(8,128)S(1)}, f32[2,24,128]{2,1,0:T(8,128)S(1)}, u32[]{:S(2)}, u32[]{:S(2)}) collective-permute-start(f32[2,24,128]{2,1,0:T(8,128)S(1)} %get-tuple-element.34), channel_id=1, source_target_pairs={{16,32},{48,64},{80,96},{112,128},{144,160},{176,192},{208,224},{2... | collective-permute-start | bytes 73736 | tf_op jit(solution)/shard_map/ppermute | solution.py:684
  78.4 14.3 %collective-permute-start.5 = (f32[2,24,128]{2,1,0:T(8,128)S(1)}, f32[2,24,128]{2,1,0:T(8,128)S(1)}, u32[]{:S(2)}, u32[]{:S(2)}) collective-permute-start(f32[2,24,128]{2,1,0:T(8,128)S(1)} %get-tuple-element.34), channel_id=1, source_target_pairs={{0,16},{32,48},{64,80},{96,112},{128,144},{160,176},{192,208},{224... | collective-permute-start | bytes 73736 | tf_op jit(solution)/shard_map/ppermute | solution.py:683

commit v2 on v1

--- a/solution.py
+++ b/solution.py
@@ -98,23 +98,35 @@
     return 1.0 / jnp.where(diagonal > 0.0, diagonal, 1.0)
 
 
-def strip_kernel(own_ref, before_ref, after_ref, up_ref, down_ref):
+def pick(even, first, second):
+    return jnp.where(even, first, second)
+
+
+def strip_row(i, own_ref, left_ref, right_ref, even):
+    if i < SIDE:
+        return pick(even, left_ref[i], right_ref[i])
+    if i < SIDE + PACK:
+        return own_ref[i - SIDE]
+    k = i - SIDE - PACK
+    return pick(even, right_ref[k], left_ref[k])
+
+
+def strip_kernel(own_ref, left_ref, right_ref, far_ref, near_ref):
+    even = lax.axis_index("wide") % 2 == 0
+    first_core = lax.axis_index("core") == 0
     for i in range(STRIP):
-        if i < SIDE:
-            row = before_ref[i]
-        elif i < SIDE + PACK:
-            row = own_ref[i - SIDE]
-        else:
-            row = after_ref[i - SIDE - PACK]
+        row = strip_row(i, own_ref, left_ref, right_ref, even)
         k, part = STRIP + i // 2, slice(HALF * (i % 2), HALF * (i % 2 + 1))
-        up_ref[i] = row[BY - 8:]
-        up_ref[k, part] = row[BY - 8 - HALF:BY - 8]
-        down_ref[i] = row[:8]
-        down_ref[k, part] = row[8:8 + HALF]
+        low, low_half = row[:8], row[8:8 + HALF]
+        high, high_half = row[BY - 8:], row[BY - 8 - HALF:BY - 8]
+        far_ref[i] = pick(first_core, low, high)
+        far_ref[k, part] = pick(first_core, low_half, high_half)
+        near_ref[i] = pick(first_core, high, low)
+        near_ref[k, part] = pick(first_core, high_half, low_half)
 
 
 def local_kernel(
-    own_ref, before_ref, after_ref, up_ref, down_ref,
+    own_ref, left_ref, right_ref, far_ref, near_ref,
     fan_ref, edge_ref,
     load1_ref, active1_ref, wx1_ref, wy1_ref, wz1_ref, diag1_ref, inv1_ref, smooth1_ref,
     load0_ref, active0_ref, wx0_ref, wy0_ref, wz0_ref, diag0_ref, inv0_ref, smooth0_ref,
@@ -122,16 +134,23 @@
 ):
     edge_rows = jnp.zeros((8 - HALF, BZ), F32)
 
+    even = lax.axis_index("wide") % 2 == 0
+    first_core = lax.axis_index("core") == 0
+
     def extended(i):
-        if i < SIDE:
-            own = before_ref[i]
-        elif i < SIDE + PACK:
-            own = own_ref[i - SIDE]
-        else:
-            own = after_ref[i - SIDE - PACK]
         k, part = STRIP + i // 2, slice(HALF * (i % 2), HALF * (i % 2 + 1))
+        far, near, far_half, near_half = far_ref[i], near_ref[i], far_ref[k, part], near_ref[k, part]
         return jnp.concatenate(
-            [edge_rows, up_ref[k, part], up_ref[i], own, down_ref[i], down_ref[k, part], edge_rows], 0
+            [
+                edge_rows,
+                pick(first_core, far_half, near_half),
+                pick(first_core, far, near),
+                strip_row(i, own_ref, left_ref, right_ref, even),
+                pick(first_core, near, far),
+                pick(first_core, near_half, far_half),
+                edge_rows,
+            ],
+            0,
         )
 
     middle = SIDE
@@ -551,7 +570,7 @@
     return [pltpu.VMEM(shape, F32)] * count
 
 
-def strip_part(own, before, after):
+def strip_part(own, odd, even):
     return pl.pallas_call(
         strip_kernel,
         out_shape=grids(2, STRIP + (STRIP + 1) // 2, 8, BZ),
@@ -559,10 +578,10 @@
         out_specs=in_vmem(2),
         compiler_params=pltpu.CompilerParams(vmem_limit_bytes=4 * 2**20),
         name="strip_part",
-    )(own, before, after)
-
-
-def local_part(own, before, after, up, down, fan):
+    )(own, odd, even)
+
+
+def local_part(own, odd, even, far, near, fan):
     middle = grids(8, MX, MY, BZ)
     middle[2] = jax.ShapeDtypeStruct((MX + 1, MY, BZ), F32)
     outs = (
@@ -579,7 +598,7 @@
         + scratch(1, MX, MY, BZ) + scratch(1, MY, BZ),
         compiler_params=pltpu.CompilerParams(vmem_limit_bytes=24 * 2**20),
         name="local_part",
-    )(own, before, after, up, down)
+    )(own, odd, even, far, near)
 
 
 def coarse_part(wide, deep, mine, other):
@@ -613,30 +632,21 @@
     )(wanted, even, odd, *kept)
 
 
-def upward(size):
-    return [(i, i + 1) for i in range(size - 1)]
-
-
-def downward(size):
-    return [(i + 1, i) for i in range(size - 1)]
-
-
 def swapped(size, start):
     pairs = [(i, i + 1) for i in range(start, size - 1, 2)]
     return pairs + [(j, i) for i, j in pairs]
 
 
-def pack_kernel(
-    source_ref, coef_ref, tops_ref, own_ref, right_ref, left_ref, tops, sems
-):
+def pack_kernel(source_ref, coef_ref, tops_ref, own_ref, odd_ref, even_ref, tops, sems):
+    odd = lax.axis_index("wide") % 2
     moves = (
         (tops_ref, tops),
         (source_ref, own_ref.at[pl.ds(0, BX)]),
         (coef_ref, own_ref.at[pl.ds(BX, BX)]),
-        (source_ref.at[pl.ds(BX - NS, NS)], right_ref.at[pl.ds(0, NS)]),
-        (coef_ref.at[pl.ds(BX - NC, NC)], right_ref.at[pl.ds(NS, NC)]),
-        (source_ref.at[pl.ds(0, NS)], left_ref.at[pl.ds(0, NS)]),
-        (coef_ref.at[pl.ds(0, NC)], left_ref.at[pl.ds(NS, NC)]),
+        (source_ref.at[pl.ds(odd * (BX - NS), NS)], odd_ref.at[pl.ds(0, NS)]),
+        (coef_ref.at[pl.ds(odd * (BX - NC), NC)], odd_ref.at[pl.ds(NS, NC)]),
+        (source_ref.at[pl.ds((1 - odd) * (BX - NS), NS)], even_ref.at[pl.ds(0, NS)]),
+        (coef_ref.at[pl.ds((1 - odd) * (BX - NC), NC)], even_ref.at[pl.ds(NS, NC)]),
     )
     copies = [pltpu.make_async_copy(*move, sems.at[i]) for i, move in enumerate(moves)]
     for copy in copies:
@@ -650,8 +660,8 @@
         column = jnp.sum(jnp.where(same, values[x:x + 1], 0.0), axis=1, keepdims=True)
         turned = jnp.where(lanes == x, column, turned)
     own_ref[PACK - 1] = turned
-    right_ref[SIDE - 1] = turned
-    left_ref[SIDE - 1] = turned
+    odd_ref[SIDE - 1] = turned
+    even_ref[SIDE - 1] = turned
     for copy in copies[1:]:
         copy.wait()
 
@@ -669,13 +679,13 @@
 
 
 def shards(wide, deep, source, conductivity, ice_cells):
-    own, right, left = pack_part(source, conductivity, ice_cells)
-    before = lax.ppermute(right, "wide", upward(wide))
-    after = lax.ppermute(left, "wide", downward(wide))
-    up, down = strip_part(own, before, after)
-    up = lax.ppermute(up, ("z", "core"), upward(2 * deep))
-    down = lax.ppermute(down, ("z", "core"), downward(2 * deep))
-    fan, edge, *kept = local_part(own, before, after, up, down, wide * deep)
+    own, odd, even = pack_part(source, conductivity, ice_cells)
+    odd = lax.ppermute(odd, "wide", swapped(wide, 1))
+    even = lax.ppermute(even, "wide", swapped(wide, 0))
+    far, near = strip_part(own, odd, even)
+    far = lax.ppermute(far, ("z", "core"), swapped(2 * deep, 1))
+    near = lax.ppermute(near, ("z", "core"), swapped(2 * deep, 0))
+    fan, edge, *kept = local_part(own, odd, even, far, near, wide * deep)
     fan = fan.reshape(wide * deep, 1, ROWS * BZ)
     mine = lax.all_to_all(fan, ("wide", "z"), 0, 0, tiled=True)
     mine = mine.reshape(wide * deep * ROWS, BZ)

time: 95.2 us -> 90.5 us (0.951)
  waiting for transfers between devices: 9.62 us -> 4.46 us
  starting transfers between devices: 23.4 us -> 27.1 us
  blocking collectives: 44 us -> 40.8 us
    ppermute x4, waiting for transfers between devices: 9.61 us -> 4.45 us  [the longest x1 2.29 us: shards(): far = lax.ppermute(far, ('z', 'core'), swapped(2 * deep, 1))]
    all_to_all x1, blocking collectives: 44 us -> 40.8 us  [shards(): mine = lax.all_to_all(fan, ('wide', 'z'), 0, 0, tiled=True)]
    ppermute x1, starting transfers between devices: 3.11 us -> 5.63 us  [shards(): other = lax.ppermute(mine, 'core', [(0, 1), (1, 0)])]
    ppermute x4, starting transfers between devices: 13.8 us -> 15 us  [the longest x1 6.56 us: shards(): even = lax.ppermute(even, 'wide', swapped(wide, 0))]
  transfers between devices with their start and end apart: 7 -> 7, of which waited for: 4 -> 2; matrix products, arithmetic and copies ran while one was open for 0% -> 0% of each run, Pallas kernels for 9% -> 9%
where the time goes in v2:
time: 90.5 us; the launch traced here: 90.2 us
  blocking collectives  40.8 us (45%)
  starting transfers between devices  27.1 us (30%)
  Pallas kernels  17.7 us (20%)
  waiting for transfers between devices  4.46 us (5%)
    all_to_all x1, blocking collectives, shards(): mine = lax.all_to_all(fan, ('wide', 'z'), 0, 0, tiled=True)  40.8 us
    pallas_call x1, Pallas kernels, coarse_part(): pl.pallas_call(functools.partial(coarse_kernel, wide, deep), out_shape=ja...  8.39 us
    ppermute x1, starting transfers between devices, shards(): even = lax.ppermute(even, 'wide', swapped(wide, 0))  6.56 us
    pallas_call x1, Pallas kernels, local_part(): pl.pallas_call(local_kernel, out_shape=outs, in_specs=in_vmem(5), out_spe...  6.05 us
    ppermute x1, starting transfers between devices, shards(): even = lax.ppermute(edge, 'wide', swapped(wide, 0))  5.81 us
    ppermute x1, starting transfers between devices, shards(): far = lax.ppermute(far, ('z', 'core'), swapped(2 * deep, 1))  5.8 us
    ppermute x1, starting transfers between devices, shards(): other = lax.ppermute(mine, 'core', [(0, 1), (1, 0)])  5.63 us
    ppermute x1, waiting for transfers between devices, shards(): far = lax.ppermute(far, ('z', 'core'), swapped(2 * deep, 1))  2.29 us
  transfers between devices with their start and end apart: 7, of which 2 were waited for; matrix products, arithmetic and copies ran while one was open for 0% of the time, Pallas kernels for 9%

profile of v2, /device:TPU:1, one launch (start us, length us, event | category | flops | bytes accessed | tf_op | source)
XLA Modules:
  0.0 90.2 jit_solution(809944031680164910)
XLA Ops:
  0.0 1.0 %pack_part.1 = (f32[17,16,128]{2,1,0:T(8,128)S(1)}, f32[14,16,128]{2,1,0:T(8,128)S(1)}, f32[14,16,128]{2,1,0:T(8,128)S(1)}) custom-call(f32[8,16,128]{2,1,0:T(8,128)} %source_ref.1, f32[8,16,128]{2,1,0:T(8,128)} %coef_ref.1, s32[8,16]{1,0:T(8,128)} %tops_ref.1), custom_call_target="tpu_custom_call" | custom-call | tf_op jit(solution)/shard_map/pack_part/pallas_call | solution.py:670
  1.0 0.7 collective-permute-start
  1.7 6.6 %collective-permute-start.1 = (f32[14,16,128]{2,1,0:T(8,128)S(1)}, f32[14,16,128]{2,1,0:T(8,128)S(1)}, u32[]{:S(2)}, u32[]{:S(2)}) collective-permute-start(f32[14,16,128]{2,1,0:T(8,128)S(1)} %get-tuple-element.30), channel_id=1, source_target_pairs={{0,16},{32,48},{64,80},{96,112},{128,144},{160,176},{192,208},{224... | collective-permute-start | bytes 344072 | tf_op jit(solution)/shard_map/ppermute | solution.py:684
  8.3 0.0 collective-permute-done.left_ref
  8.3 2.2 %collective-permute-done.1.right_ref = f32[14,16,128]{2,1,0:T(8,128)S(1)} collective-permute-done((f32[14,16,128]{2,1,0:T(8,128)S(1)}, f32[14,16,128]{2,1,0:T(8,128)S(1)}, u32[]{:S(2)}, u32[]{:S(2)}) %collective-permute-start.1) | collective-permute-done | bytes 114720 | tf_op jit(solution)/shard_map/ppermute | solution.py:684
  10.4 0.1 strip_part.1
  10.5 5.8 %collective-permute-start.2 = (f32[68,8,128]{2,1,0:T(8,128)S(1)}, f32[68,8,128]{2,1,0:T(8,128)S(1)}, u32[]{:S(2)}, u32[]{:S(2)}) collective-permute-start(f32[68,8,128]{2,1,0:T(8,128)S(1)} %get-tuple-element.31), channel_id=1, source_target_pairs={{1,2},{3,4},{5,6},{7,8},{9,10},{11,12},{13,14},{2,1},{4,3},{6,5},{... | collective-permute-start | bytes 835592 | tf_op jit(solution)/shard_map/ppermute | solution.py:686
  16.3 1.9 %collective-permute-start.3 = (f32[68,8,128]{2,1,0:T(8,128)S(1)}, f32[68,8,128]{2,1,0:T(8,128)S(1)}, u32[]{:S(2)}, u32[]{:S(2)}) collective-permute-start(f32[68,8,128]{2,1,0:T(8,128)S(1)} %get-tuple-element.32), channel_id=1, source_target_pairs={{0,1},{2,3},{4,5},{6,7},{8,9},{10,11},{12,13},{14,15},{1,0},{3,2},... | collective-permute-start | bytes 835592 | tf_op jit(solution)/shard_map/ppermute | solution.py:687
  18.3 2.3 %collective-permute-done.2.far_ref = f32[68,8,128]{2,1,0:T(8,128)S(1)} collective-permute-done((f32[68,8,128]{2,1,0:T(8,128)S(1)}, f32[68,8,128]{2,1,0:T(8,128)S(1)}, u32[]{:S(2)}, u32[]{:S(2)}) %collective-permute-start.2) | collective-permute-done | bytes 278560 | tf_op jit(solution)/shard_map/ppermute | solution.py:686
  20.5 0.0 collective-permute-done.3.near_ref
  20.5 6.0 %local_part.1 = (f32[1280,128]{1,0:T(8,128)S(1)}, f32[2,24,128]{2,1,0:T(8,128)S(1)}, f32[12,24,128]{2,1,0:T(8,128)S(1)}, f32[12,24,128]{2,1,0:T(8,128)S(1)}, f32...) custom-call(f32[17,16,128]{2,1,0:T(8,128)S(1)} %get-tuple-element.28, ...), custom_call_target="tpu_custom_call" | custom-call | tf_op jit(solution)/shard_map/local_part/pallas_call | solution.py:592
  26.6 40.8 %all_to_all.5 = f32[256,1,640]{2,1,0:T(1,128)S(1)} all-to-all(f32[256,1,640]{2,1,0:T(1,128)S(1)} %bitcast.4), channel_id=1, replica_groups=mesh['wide'=32,'z'=8,'core'=2] {'wide','z'}, dimensions={0} | all-to-all | bytes 1310720 | tf_op jit(solution)/shard_map/all_to_all | solution.py:690
  67.4 5.6 %collective-permute-start.4 = (f32[1280,128]{1,0:T(8,128)S(1)}, f32[1280,128]{1,0:T(8,128)S(1)}, u32[]{:S(2)}, u32[]{:S(2)}) collective-permute-start(f32[1280,128]{1,0:T(8,128)S(1)} %bitcast.2), channel_id=1, source_target_pairs={{0,1},{1,0},{2,3},{3,2},{4,5},{5,4},{6,7},{7,6},{8,9},{9,8},{10,11... | collective-permute-start | bytes 1966088 | tf_op jit(solution)/shard_map/ppermute | solution.py:692
  73.1 0.7 collective-permute-start.6
  73.7 5.8 %collective-permute-start.5 = (f32[2,24,128]{2,1,0:T(8,128)S(1)}, f32[2,24,128]{2,1,0:T(8,128)S(1)}, u32[]{:S(2)}, u32[]{:S(2)}) collective-permute-start(f32[2,24,128]{2,1,0:T(8,128)S(1)} %get-tuple-element.34), channel_id=1, source_target_pairs={{0,16},{32,48},{64,80},{96,112},{128,144},{160,176},{192,208},{224... | collective-permute-start | bytes 73736 | tf_op jit(solution)/shard_map/ppermute | solution.py:693
  79.5 0.0 collective-permute-done.4.other_ref
  79.5 8.4 %coarse_part.1.wanted = f32[24,128]{1,0:T(8,128)S(1)} custom-call(f32[1280,128]{1,0:T(8,128)S(1)} %bitcast.3, f32[1280,128]{1,0:T(8,128)S(1)} %collective-permute-done.4.other_ref), custom_call_target="tpu_custom_call" | custom-call | flops 32768000 | bytes 4194304 | tf_op jit(solution)/shard_map/coarse_part/pallas_call | solution.py:608
  87.9 0.0 collective-permute-done.6.odd_ref
  88.0 0.0 collective-permute-done.5.even_ref
  88.0 2.2 %finish_part.1 = f32[8,16,128]{2,1,0:T(8,128)} custom-call(f32[24,128]{1,0:T(8,128)S(1)} %coarse_part.1.wanted, f32[2,24,128]{2,1,0:T(8,128)S(1)} %collective-permute-done.5.even_ref, f32[2,24,128]{2,1,0:T(8,128)S(1)} %collective-permute-done.6.odd_ref, f32[12,24,128]{2,1,0:T(8,128)S(1)} %get-tuple-element.35.load1_ref, ...), custom_call_target="tpu_custom_call" | custom-call | tf_op jit(solution)/shard_map/finish_part/pallas_call | solution.py:623
Async XLA Ops:
  1.0 7.2 %collective-permute-start = (f32[14,16,128]{2,1,0:T(8,128)S(1)}, f32[14,16,128]{2,1,0:T(8,128)S(1)}, u32[]{:S(2)}, u32[]{:S(2)}) collective-permute-start(f32[14,16,128]{2,1,0:T(8,128)S(1)} %get-tuple-element.29), channel_id=1, source_target_pairs={{16,32},{48,64},{80,96},{112,128},{144,160},{176,192},{208,224},{2... | collective-permute-start | bytes 344072 | tf_op jit(solution)/shard_map/ppermute | solution.py:683
  1.7 8.7 %collective-permute-start.1 = (f32[14,16,128]{2,1,0:T(8,128)S(1)}, f32[14,16,128]{2,1,0:T(8,128)S(1)}, u32[]{:S(2)}, u32[]{:S(2)}) collective-permute-start(f32[14,16,128]{2,1,0:T(8,128)S(1)} %get-tuple-element.30), channel_id=1, source_target_pairs={{0,16},{32,48},{64,80},{96,112},{128,144},{160,176},{192,208},{224... | collective-permute-start | bytes 344072 | tf_op jit(solution)/shard_map/ppermute | solution.py:684
  10.5 10.0 %collective-permute-start.2 = (f32[68,8,128]{2,1,0:T(8,128)S(1)}, f32[68,8,128]{2,1,0:T(8,128)S(1)}, u32[]{:S(2)}, u32[]{:S(2)}) collective-permute-start(f32[68,8,128]{2,1,0:T(8,128)S(1)} %get-tuple-element.31), channel_id=1, source_target_pairs={{1,2},{3,4},{5,6},{7,8},{9,10},{11,12},{13,14},{2,1},{4,3},{6,5},{... | collective-permute-start | bytes 835592 | tf_op jit(solution)/shard_map/ppermute | solution.py:686
  16.3 4.2 %collective-permute-start.3 = (f32[68,8,128]{2,1,0:T(8,128)S(1)}, f32[68,8,128]{2,1,0:T(8,128)S(1)}, u32[]{:S(2)}, u32[]{:S(2)}) collective-permute-start(f32[68,8,128]{2,1,0:T(8,128)S(1)} %get-tuple-element.32), channel_id=1, source_target_pairs={{0,1},{2,3},{4,5},{6,7},{8,9},{10,11},{12,13},{14,15},{1,0},{3,2},... | collective-permute-start | bytes 835592 | tf_op jit(solution)/shard_map/ppermute | solution.py:687
  67.4 12.1 %collective-permute-start.4 = (f32[1280,128]{1,0:T(8,128)S(1)}, f32[1280,128]{1,0:T(8,128)S(1)}, u32[]{:S(2)}, u32[]{:S(2)}) collective-permute-start(f32[1280,128]{1,0:T(8,128)S(1)} %bitcast.2), channel_id=1, source_target_pairs={{0,1},{1,0},{2,3},{3,2},{4,5},{5,4},{6,7},{7,6},{8,9},{9,8},{10,11... | collective-permute-start | bytes 1966088 | tf_op jit(solution)/shard_map/ppermute | solution.py:692
  73.1 14.9 %collective-permute-start.6 = (f32[2,24,128]{2,1,0:T(8,128)S(1)}, f32[2,24,128]{2,1,0:T(8,128)S(1)}, u32[]{:S(2)}, u32[]{:S(2)}) collective-permute-start(f32[2,24,128]{2,1,0:T(8,128)S(1)} %get-tuple-element.34), channel_id=1, source_target_pairs={{16,32},{48,64},{80,96},{112,128},{144,160},{176,192},{208,224},{2... | collective-permute-start | bytes 73736 | tf_op jit(solution)/shard_map/ppermute | solution.py:694
  73.7 14.2 %collective-permute-start.5 = (f32[2,24,128]{2,1,0:T(8,128)S(1)}, f32[2,24,128]{2,1,0:T(8,128)S(1)}, u32[]{:S(2)}, u32[]{:S(2)}) collective-permute-start(f32[2,24,128]{2,1,0:T(8,128)S(1)} %get-tuple-element.34), channel_id=1, source_target_pairs={{0,16},{32,48},{64,80},{96,112},{128,144},{160,176},{192,208},{224... | collective-permute-start | bytes 73736 | tf_op jit(solution)/shard_map/ppermute | solution.py:693

commit v3 on v2

--- a/solution.py
+++ b/solution.py
@@ -29,7 +29,8 @@
 MX, MY = EX // 2, EY // 2
 TX, TY = 12, 32
 X0, Y0 = 6, 8
-BLOCK = 16
+BLOCK = 4
+SETUP = 2
 ROWS = 5
 
 
@@ -306,55 +307,63 @@
     lax.fori_loop(0, fan_ref.shape[0] // (8 * ROWS), fan, 0)
 
 
+def block_transpose(values, lanes):
+    odd, high = (lanes & 32) != 0, (lanes & 64) != 0
+    turn = [jnp.where(odd, values[(j + 1) % 4], values[j]) for j in range(4)]
+    turn = [jnp.where(high, turn[(j + 2) % 4], turn[j]) for j in range(4)]
+    skew = [shift(turn[(4 - d) % 4], -32 * d, 1) if d else turn[0] for d in range(4)]
+    back = [jnp.where(odd, skew[(j + 3) % 4], skew[j]) for j in range(4)]
+    return [jnp.where(high, back[(j + 2) % 4], back[j]) for j in range(4)]
+
+
 def coarse_kernel(
     wide, deep, mine_ref, other_ref, wanted,
     coef, active, wx, wy, wz, diag, residual, image, slope, direction, solution,
 ):
     count = 2 * wide
+    planes = count // 4
+    block = min(BLOCK, planes)
     vector = (deep, BZ)
-    lanes = lane_index((BLOCK, deep, BZ))
+    lanes = lane_index(vector)
     zero = jnp.zeros(vector, F32)
-    pad = 2
-
-    def pair(first, second):
-        return jnp.stack([first, second], 1)
+    highest = (lanes & 31) == 31
+    last_row = lax.broadcasted_iota(jnp.int32, vector, 0) == deep - 1
+    last_block = lanes >= 96
 
     def y_after(value):
-        turned = shift(value, -32, 3)
-        first, second = turned[:, 0], turned[:, 1]
-        inside = lanes < 96
-        return pair(jnp.where(inside, first, second), jnp.where(inside, second, shift(first, -1, 1)))
+        return jnp.concatenate([value[:, 1:], shift(value[:, :1], -1, 2)], 1)
 
     def y_before(value):
-        turned = shift(value, 32, 3)
-        first, second = turned[:, 0], turned[:, 1]
-        inside = lanes >= 32
-        return pair(jnp.where(inside, first, shift(second, 1, 1)), jnp.where(inside, second, first))
-
-    for ref, spare in ((residual, (*range(pad), *range(count + pad, count + 2 * pad))), (image, (count,)), (slope, (count,))):
-        for x in spare:
-            ref[x] = jnp.zeros((2, *vector), F32)
+        return jnp.concatenate([shift(value[:, 7:], 1, 2), value[:, :7]], 1)
 
     stride = deep * ROWS
-    flat = lane_index(vector)
-    low = (flat & 16) == 0
-    layer = ((flat & 31) * 4).astype(F32)
+    low = (lanes & 16) == 0
+    layer = ((lanes & 31) * 4).astype(F32)
 
     def unpack(refs):
         def body(w, slot):
             for c in range(2):
-                top, *rows = (
-                    refs[c][pl.ds(w * stride + k, deep, stride=ROWS), :] for k in (4, 0, 1, 2, 3)
-                )
-                tall = (
-                    jnp.where(low, top, shift(top, 16, 1)), jnp.where(low, shift(top, -16, 1), top)
-                )
-                for i in range(2):
-                    residual[2 * w + i + pad, c] = rows[i]
-                    coef[2 * w + i, c] = rows[2 + i]
-                    active[2 * w + i, c] = (layer < tall[i]).astype(F32)
-
-        loop(0, wide, 2, body)
+                def turned(k):
+                    return block_transpose(
+                        [
+                            refs[c][pl.ds((q * (wide // 4) + w) * stride + k, deep, stride=ROWS), :]
+                            for q in range(4)
+                        ],
+                        lanes,
+                    )
+
+                loads, coefs, tops = (turned(0), turned(1)), (turned(2), turned(3)), turned(4)
+                for y in range(4):
+                    tall = (
+                        jnp.where(low, tops[y], shift(tops[y], 16, 1)),
+                        jnp.where(low, shift(tops[y], -16, 1), tops[y]),
+                    )
+                    for i in range(2):
+                        residual[2 * w + i, 4 * c + y] = loads[i][y]
+                        coef[2 * w + i, 4 * c + y] = coefs[i][y]
+                        active[2 * w + i, 4 * c + y] = (layer < tall[i]).astype(F32)
+
+        loop(0, planes // 2, 1, body)
 
     own_core = lax.axis_index("core")
 
@@ -366,40 +375,33 @@
     def _():
         unpack((other_ref, mine_ref))
 
-    lanes4 = lane_index((BLOCK, 2, deep, BZ))
-    highest = (lanes4 & 31) == 31
-    shape4 = (BLOCK, 2, deep, BZ)
-    last_y = (
-        (lanes4 >= 96)
-        & (lax.broadcasted_iota(jnp.int32, shape4, 1) == 1)
-        & (lax.broadcasted_iota(jnp.int32, shape4, 2) == deep - 1)
-    )
-
     def coarse_weight(a, b):
         return 8.0 * a * b / (a + b)
 
-    coef[count] = jnp.zeros((2, *vector), F32)
-    active[count] = jnp.zeros((2, *vector), F32)
-    wx[0] = jnp.zeros((2, *vector), F32)
+    coef[planes] = jnp.where(last_block, 0.0, shift(coef[0], -32, 2))
+    active[planes] = jnp.where(last_block, 0.0, shift(active[0], -32, 2))
 
     def setup(i, face):
-        x = i * BLOCK
-        coefs, masks = coef[pl.ds(x, BLOCK + 1)], active[pl.ds(x, BLOCK + 1)]
-        here, mask = coefs[:BLOCK], masks[:BLOCK]
+        x = i * SETUP
+        coefs, masks = coef[pl.ds(x, SETUP + 1)], active[pl.ds(x, SETUP + 1)]
+        here, mask = coefs[:SETUP], masks[:SETUP]
         after = coarse_weight(here, coefs[1:])
         before = jnp.concatenate([face, after[:-1]], 0)
-        beside = jnp.where(last_y, 0.0, coarse_weight(here, y_after(here)))
+        beside = coarse_weight(here, y_after(here))
+        beside = jnp.concatenate([beside[:, :7], jnp.where(last_row, 0.0, beside[:, 7:])], 1)
         above = coarse_weight(here, shift(here, -1, 3))
         inner = jnp.where(highest, 0.0, above)
         top = jnp.where(highest, 4.0 * here, above)
         total = after + before + beside + y_before(beside) + top + shift(inner, 1, 3)
-        diag[pl.ds(x, BLOCK)] = mask * total
-        wx[pl.ds(x + 1, BLOCK)] = after * (mask * masks[1:])
-        wy[pl.ds(x, BLOCK)] = beside * (mask * y_after(mask))
-        wz[pl.ds(x, BLOCK)] = inner * (mask * shift(mask, -1, 3))
+        diag[pl.ds(x, SETUP)] = mask * total
+        wx[pl.ds(x + 1, SETUP)] = after * (mask * masks[1:])
+        wy[pl.ds(x, SETUP)] = beside * (mask * y_after(mask))
+        wz[pl.ds(x, SETUP)] = inner * (mask * shift(mask, -1, 3))
         return after[-1:]
 
-    lax.fori_loop(0, count // BLOCK, setup, jnp.zeros((1, 2, *vector), F32))
+    closing = coarse_weight(coef[planes - 1:planes], coef[planes:planes + 1])
+    lax.fori_loop(0, planes // SETUP, setup, shift(closing, 32, 3))
+    wx[0] = shift(wx[planes], 32, 2)
 
     def whole(total):
         return jnp.sum(jnp.sum(total, axis=0, keepdims=True), axis=1, keepdims=True)
@@ -407,7 +409,14 @@
     def fold(total, value):
         return total + jnp.sum(value, axis=(0, 1))
 
-    first = 2 * lax.axis_index("wide")
+    first_x = 2 * lax.axis_index("wide") - 2
+    position = 2 * lax.axis_index("z") + own_core
+    xs = [jnp.clip(first_x + i, 0, count - 1) for i in range(6)]
+    groups = [jnp.clip(position + j - 1, 0, 2 * deep - 1) for j in range(3)]
+    direction[...] = jnp.zeros(direction.shape, F32)
+    solution[...] = jnp.zeros(solution.shape, F32)
+    wanted[...] = jnp.zeros(wanted.shape, F32)
+
     ratio = scale = norm = jnp.zeros((1, 1), F32)
     for iteration in range(ITERS):
         start = iteration == 0
@@ -415,56 +424,70 @@
             wide_ratio = jnp.broadcast_to(ratio, vector)[None, None]
             wide_scale = jnp.broadcast_to(scale, vector)[None, None]
 
-        def renew(x, size):
-            value = residual[pl.ds(x + pad, size)]
+        def renew(x, size, keep=True):
+            value = residual[pl.ds(x, size)]
             if start:
                 return value
             slope_here = image[pl.ds(x, size)]
             if iteration > 1:
                 slope_here = slope_here + wide_ratio * slope[pl.ds(x, size)]
-            if iteration < ITERS - 1:
-                slope[pl.ds(x, size)] = slope_here
             value = value - wide_scale * slope_here
-            residual[pl.ds(x + pad, size)] = value
+            if keep:
+                if iteration < ITERS - 1:
+                    slope[pl.ds(x, size)] = slope_here
+                residual[pl.ds(x, size)] = value
             return value
 
-        def apply(i, carry):
-            x = i * BLOCK
+        def apply(x, carry, later):
             norm_sum, image_sum, last = carry
-            grown = jnp.concatenate([last, renew(x + 1, BLOCK)], 0)
-            before, here, after = grown[:BLOCK], grown[1:BLOCK + 1], grown[2:]
-            weight_y, weight_z = wy[pl.ds(x, BLOCK)], wz[pl.ds(x, BLOCK)]
-            faces = wx[pl.ds(x, BLOCK + 1)]
+            grown = jnp.concatenate([last, later], 0)
+            before, here, after = grown[:block], grown[1:block + 1], grown[2:]
+            weight_y, weight_z = wy[pl.ds(x, block)], wz[pl.ds(x, block)]
+            faces = wx[pl.ds(x, block + 1)]
             coupled = faces[1:] * after + faces[:-1] * before
             coupled = coupled + weight_y * y_after(here) + y_before(weight_y * here)
             coupled = coupled + weight_z * shift(here, -1, 3) + shift(weight_z * here, 1, 3)
-            value = diag[pl.ds(x, BLOCK)] * here - coupled
-            image[pl.ds(x, BLOCK)] = value
-            return fold(norm_sum, here * here), fold(image_sum, here * value), grown[BLOCK:]
-
-        opening = jnp.concatenate([jnp.zeros((1, 2, *vector), F32), renew(0, 1)], 0)
-        norm_sum, image_sum, _ = lax.fori_loop(0, count // BLOCK, apply, (zero, zero, opening))
+            value = diag[pl.ds(x, block)] * here - coupled
+            image[pl.ds(x, block)] = value
+            return fold(norm_sum, here * here), fold(image_sum, here * value), grown[block:]
+
+        before_first = shift(renew(planes - 1, 1, False), 32, 3)
+        opening = renew(0, 1)
+        carry = (zero, zero, jnp.concatenate([before_first, opening], 0))
+
+        def turn(i, carry):
+            x = i * block
+            return apply(x, carry, renew(x + 1, block))
+
+        carry = lax.fori_loop(0, planes // block - 1, turn, carry)
+        x = planes - block
+        beyond = shift(residual[0:1], -32, 3)
+        if block > 1:
+            beyond = jnp.concatenate([renew(x + 1, block - 1), beyond], 0)
+        norm_sum, image_sum, _ = apply(x, carry, beyond)
+        for i in range(6):
+            for j in range(3):
+                for y in range(4):
+                    row = 16 * i + 4 * j + y
+                    wanted[row:row + 1, :] = residual[
+                        lax.rem(xs[i], planes), 4 * (groups[j] & 1) + y, pl.ds(groups[j] >> 1, 1), :
+                    ]
         fresh, curvature = whole(norm_sum), whole(image_sum)
-        here = residual[pl.ds(first, 6)]
+        here = wanted[...]
         if start:
             scale = fresh / curvature
-            direction[...] = here
-            solution[...] = jnp.broadcast_to(scale, vector)[None, None] * here
         else:
             ratio = fresh / norm
             scale = fresh / (curvature - ratio * fresh / scale)
-            here = here + jnp.broadcast_to(ratio, vector)[None, None] * direction[...]
-            direction[...] = here
-            solution[...] = solution[...] + jnp.broadcast_to(scale, vector)[None, None] * here
+            here = here + ratio * direction[...]
+        direction[...] = here
+        solution[...] = solution[...] + scale * here
         norm = fresh
 
-    position = 2 * lax.axis_index("z") + own_core
-    wanted[...] = jnp.zeros(wanted.shape, F32)
-    for j in range(3):
-        group = jnp.clip(position + j - 1, 0, 2 * deep - 1)
-        core, row = group & 1, group >> 1
-        for i in range(6):
-            wanted[3 * i + j:3 * i + j + 1, :] = solution[i, core, pl.ds(row, 1), :]
+    columns = lane_index((16, BZ))
+    for i in range(6):
+        own_block = columns // 32 == xs[i] // planes
+        wanted[16 * i:16 * i + 16] = jnp.where(own_block, solution[16 * i:16 * i + 16], 0.0)
 
 
 def finish_kernel(
@@ -474,9 +497,8 @@
     out_ref,
     spread, guess1, update1, second1, children, guess0, update0, second0,
 ):
-    entry = lax.broadcasted_iota(jnp.int32, (BZ, 4 * BZ), 0)
-    columns = lane_index((BZ, 4 * BZ))
-    chosen = entry == (columns // BZ) * 32 + (columns % BZ) // 4
+    entry = lax.broadcasted_iota(jnp.int32, (BZ, BZ), 0)
+    chosen = entry % 32 == lane_index((BZ, BZ)) // 4
     spread[...] = jnp.dot(
         wanted[...], chosen.astype(F32), precision=lax.Precision.HIGHEST, preferred_element_type=F32
     )
@@ -484,8 +506,7 @@
     for i in range(6):
         rows = []
         for y in range(12):
-            r, c = 3 * i + y // 4, y % 4
-            row = spread[r:r + 1, c * BZ:(c + 1) * BZ]
+            row = spread[16 * i + y:16 * i + y + 1]
             rows.append(jnp.broadcast_to(row, (2, BZ)))
         parent = jnp.concatenate(rows, 0)
         for x in (2 * i, 2 * i + 1):
@@ -603,16 +624,16 @@
 
 def coarse_part(wide, deep, mine, other):
     count = 2 * wide
-    tile = (2, deep, BZ)
+    planes = count // 4
+    tile = (8, deep, BZ)
     work = count * 2 * deep * BZ
     return pl.pallas_call(
         functools.partial(coarse_kernel, wide, deep),
-        out_shape=jax.ShapeDtypeStruct((24, BZ), F32),
+        out_shape=jax.ShapeDtypeStruct((96, BZ), F32),
         in_specs=in_vmem(2),
         out_specs=pl.BlockSpec(memory_space=pltpu.VMEM),
-        scratch_shapes=scratch(3, count + 1, *tile)
-        + scratch(3, count, *tile) + scratch(1, count + 4, *tile) + scratch(2, count + 1, *tile)
-        + scratch(2, 6, *tile),
+        scratch_shapes=scratch(3, planes + 1, *tile) + scratch(6, planes, *tile)
+        + scratch(2, 96, BZ),
         compiler_params=pltpu.CompilerParams(vmem_limit_bytes=16 * 2**20),
         cost_estimate=pl.CostEstimate(flops=250 * work, bytes_accessed=8 * work * 4, transcendentals=0),
         name="coarse_part",
@@ -625,7 +646,7 @@
         out_shape=jax.ShapeDtypeStruct((BX, BY, BZ), F32),
         in_specs=in_vmem(3 + len(kept)),
         out_specs=pl.BlockSpec(memory_space=pltpu.VMEM),
-        scratch_shapes=scratch(1, 24, 4 * BZ)
+        scratch_shapes=scratch(1, 96, BZ)
         + scratch(3, MX, MY, BZ) + scratch(1, 2, EY, BZ) + scratch(3, TX, TY, BZ),
         compiler_params=pltpu.CompilerParams(vmem_limit_bytes=8 * 2**20),
         name="finish_part",

time: 90.5 us -> 89.3 us (0.987)
  Pallas kernels: 17.7 us -> 16.5 us
    pallas_call x1, Pallas kernels: 8.39 us -> 7.21 us  [coarse_part(): pl.pallas_call(functools.partial(coarse_kernel, wide, deep), out_shape=ja...]
  transfers between devices with their start and end apart: 7 -> 7, of which waited for: 2 -> 2; matrix products, arithmetic and copies ran while one was open for 0% -> 0% of each run, Pallas kernels for 9% -> 8%
where the time goes in v3:
time: 89.3 us; the launch traced here: 88.9 us
  blocking collectives  40.8 us (46%)
  starting transfers between devices  27.1 us (30%)
  Pallas kernels  16.5 us (18%)
  waiting for transfers between devices  4.46 us (5%)
    all_to_all x1, blocking collectives, shards(): mine = lax.all_to_all(fan, ('wide', 'z'), 0, 0, tiled=True)  40.8 us
    pallas_call x1, Pallas kernels, coarse_part(): pl.pallas_call(functools.partial(coarse_kernel, wide, deep), out_shape=ja...  7.21 us
    ppermute x1, starting transfers between devices, shards(): even = lax.ppermute(even, 'wide', swapped(wide, 0))  6.56 us
    pallas_call x1, Pallas kernels, local_part(): pl.pallas_call(local_kernel, out_shape=outs, in_specs=in_vmem(5), out_spe...  6.05 us
    ppermute x1, starting transfers between devices, shards(): even = lax.ppermute(edge, 'wide', swapped(wide, 0))  5.81 us
    ppermute x1, starting transfers between devices, shards(): far = lax.ppermute(far, ('z', 'core'), swapped(2 * deep, 1))  5.8 us
    ppermute x1, starting transfers between devices, shards(): other = lax.ppermute(mine, 'core', [(0, 1), (1, 0)])  5.63 us
    ppermute x1, waiting for transfers between devices, shards(): far = lax.ppermute(far, ('z', 'core'), swapped(2 * deep, 1))  2.29 us
  transfers between devices with their start and end apart: 7, of which 2 were waited for; matrix products, arithmetic and copies ran while one was open for 0% of the time, Pallas kernels for 8%

profile of v3, /device:TPU:1, one launch (start us, length us, event | category | flops | bytes accessed | tf_op | source)
XLA Modules:
  0.0 88.9 jit_solution(12483124306509569647)
XLA Ops:
  0.0 1.0 %pack_part.1 = (f32[17,16,128]{2,1,0:T(8,128)S(1)}, f32[14,16,128]{2,1,0:T(8,128)S(1)}, f32[14,16,128]{2,1,0:T(8,128)S(1)}) custom-call(f32[8,16,128]{2,1,0:T(8,128)} %source_ref.1, f32[8,16,128]{2,1,0:T(8,128)} %coef_ref.1, s32[8,16]{1,0:T(8,128)} %tops_ref.1), custom_call_target="tpu_custom_call" | custom-call | tf_op jit(solution)/shard_map/pack_part/pallas_call | solution.py:691
  1.0 0.7 collective-permute-start
  1.7 6.6 %collective-permute-start.1 = (f32[14,16,128]{2,1,0:T(8,128)S(1)}, f32[14,16,128]{2,1,0:T(8,128)S(1)}, u32[]{:S(2)}, u32[]{:S(2)}) collective-permute-start(f32[14,16,128]{2,1,0:T(8,128)S(1)} %get-tuple-element.30), channel_id=1, source_target_pairs={{0,16},{32,48},{64,80},{96,112},{128,144},{160,176},{192,208},{224... | collective-permute-start | bytes 344072 | tf_op jit(solution)/shard_map/ppermute | solution.py:705
  8.3 0.0 collective-permute-done.left_ref
  8.3 2.2 %collective-permute-done.1.right_ref = f32[14,16,128]{2,1,0:T(8,128)S(1)} collective-permute-done((f32[14,16,128]{2,1,0:T(8,128)S(1)}, f32[14,16,128]{2,1,0:T(8,128)S(1)}, u32[]{:S(2)}, u32[]{:S(2)}) %collective-permute-start.1) | collective-permute-done | bytes 114720 | tf_op jit(solution)/shard_map/ppermute | solution.py:705
  10.4 0.1 strip_part.1
  10.5 5.8 %collective-permute-start.2 = (f32[68,8,128]{2,1,0:T(8,128)S(1)}, f32[68,8,128]{2,1,0:T(8,128)S(1)}, u32[]{:S(2)}, u32[]{:S(2)}) collective-permute-start(f32[68,8,128]{2,1,0:T(8,128)S(1)} %get-tuple-element.31), channel_id=1, source_target_pairs={{1,2},{3,4},{5,6},{7,8},{9,10},{11,12},{13,14},{2,1},{4,3},{6,5},{... | collective-permute-start | bytes 835592 | tf_op jit(solution)/shard_map/ppermute | solution.py:707
  16.3 1.9 %collective-permute-start.3 = (f32[68,8,128]{2,1,0:T(8,128)S(1)}, f32[68,8,128]{2,1,0:T(8,128)S(1)}, u32[]{:S(2)}, u32[]{:S(2)}) collective-permute-start(f32[68,8,128]{2,1,0:T(8,128)S(1)} %get-tuple-element.32), channel_id=1, source_target_pairs={{0,1},{2,3},{4,5},{6,7},{8,9},{10,11},{12,13},{14,15},{1,0},{3,2},... | collective-permute-start | bytes 835592 | tf_op jit(solution)/shard_map/ppermute | solution.py:708
  18.3 2.3 %collective-permute-done.2.far_ref = f32[68,8,128]{2,1,0:T(8,128)S(1)} collective-permute-done((f32[68,8,128]{2,1,0:T(8,128)S(1)}, f32[68,8,128]{2,1,0:T(8,128)S(1)}, u32[]{:S(2)}, u32[]{:S(2)}) %collective-permute-start.2) | collective-permute-done | bytes 278560 | tf_op jit(solution)/shard_map/ppermute | solution.py:707
  20.5 0.0 collective-permute-done.3.near_ref
  20.5 6.0 %local_part.1 = (f32[1280,128]{1,0:T(8,128)S(1)}, f32[2,24,128]{2,1,0:T(8,128)S(1)}, f32[12,24,128]{2,1,0:T(8,128)S(1)}, f32[12,24,128]{2,1,0:T(8,128)S(1)}, f32...) custom-call(f32[17,16,128]{2,1,0:T(8,128)S(1)} %get-tuple-element.28, ...), custom_call_target="tpu_custom_call" | custom-call | tf_op jit(solution)/shard_map/local_part/pallas_call | solution.py:613
  26.6 40.8 %all_to_all.5 = f32[256,1,640]{2,1,0:T(1,128)S(1)} all-to-all(f32[256,1,640]{2,1,0:T(1,128)S(1)} %bitcast.4), channel_id=1, replica_groups=mesh['wide'=32,'z'=8,'core'=2] {'wide','z'}, dimensions={0} | all-to-all | bytes 1310720 | tf_op jit(solution)/shard_map/all_to_all | solution.py:711
  67.4 5.6 %collective-permute-start.4 = (f32[1280,128]{1,0:T(8,128)S(1)}, f32[1280,128]{1,0:T(8,128)S(1)}, u32[]{:S(2)}, u32[]{:S(2)}) collective-permute-start(f32[1280,128]{1,0:T(8,128)S(1)} %bitcast.2), channel_id=1, source_target_pairs={{0,1},{1,0},{2,3},{3,2},{4,5},{5,4},{6,7},{7,6},{8,9},{9,8},{10,11... | collective-permute-start | bytes 1966088 | tf_op jit(solution)/shard_map/ppermute | solution.py:713
  73.1 0.7 collective-permute-start.6
  73.7 5.8 %collective-permute-start.5 = (f32[2,24,128]{2,1,0:T(8,128)S(1)}, f32[2,24,128]{2,1,0:T(8,128)S(1)}, u32[]{:S(2)}, u32[]{:S(2)}) collective-permute-start(f32[2,24,128]{2,1,0:T(8,128)S(1)} %get-tuple-element.34), channel_id=1, source_target_pairs={{0,16},{32,48},{64,80},{96,112},{128,144},{160,176},{192,208},{224... | collective-permute-start | bytes 73736 | tf_op jit(solution)/shard_map/ppermute | solution.py:714
  79.5 0.0 collective-permute-done.4.other_ref
  79.5 7.2 %coarse_part.1.wanted = f32[96,128]{1,0:T(8,128)S(1)} custom-call(f32[1280,128]{1,0:T(8,128)S(1)} %bitcast.3, f32[1280,128]{1,0:T(8,128)S(1)} %collective-permute-done.4.other_ref), custom_call_target="tpu_custom_call" | custom-call | flops 32768000 | bytes 4194304 | tf_op jit(solution)/shard_map/coarse_part/pallas_call | solution.py:630
  86.8 0.0 collective-permute-done.6.odd_ref
  86.8 0.0 collective-permute-done.5.even_ref
  86.8 2.1 %finish_part.1 = f32[8,16,128]{2,1,0:T(8,128)} custom-call(f32[96,128]{1,0:T(8,128)S(1)} %coarse_part.1.wanted, f32[2,24,128]{2,1,0:T(8,128)S(1)} %collective-permute-done.5.even_ref, f32[2,24,128]{2,1,0:T(8,128)S(1)} %collective-permute-done.6.odd_ref, f32[12,24,128]{2,1,0:T(8,128)S(1)} %get-tuple-element.35.load1_ref, ...), custom_call_target="tpu_custom_call" | custom-call | tf_op jit(solution)/shard_map/finish_part/pallas_call | solution.py:644
Async XLA Ops:
  1.0 7.2 %collective-permute-start = (f32[14,16,128]{2,1,0:T(8,128)S(1)}, f32[14,16,128]{2,1,0:T(8,128)S(1)}, u32[]{:S(2)}, u32[]{:S(2)}) collective-permute-start(f32[14,16,128]{2,1,0:T(8,128)S(1)} %get-tuple-element.29), channel_id=1, source_target_pairs={{16,32},{48,64},{80,96},{112,128},{144,160},{176,192},{208,224},{2... | collective-permute-start | bytes 344072 | tf_op jit(solution)/shard_map/ppermute | solution.py:704
  1.7 8.7 %collective-permute-start.1 = (f32[14,16,128]{2,1,0:T(8,128)S(1)}, f32[14,16,128]{2,1,0:T(8,128)S(1)}, u32[]{:S(2)}, u32[]{:S(2)}) collective-permute-start(f32[14,16,128]{2,1,0:T(8,128)S(1)} %get-tuple-element.30), channel_id=1, source_target_pairs={{0,16},{32,48},{64,80},{96,112},{128,144},{160,176},{192,208},{224... | collective-permute-start | bytes 344072 | tf_op jit(solution)/shard_map/ppermute | solution.py:705
  10.5 10.0 %collective-permute-start.2 = (f32[68,8,128]{2,1,0:T(8,128)S(1)}, f32[68,8,128]{2,1,0:T(8,128)S(1)}, u32[]{:S(2)}, u32[]{:S(2)}) collective-permute-start(f32[68,8,128]{2,1,0:T(8,128)S(1)} %get-tuple-element.31), channel_id=1, source_target_pairs={{1,2},{3,4},{5,6},{7,8},{9,10},{11,12},{13,14},{2,1},{4,3},{6,5},{... | collective-permute-start | bytes 835592 | tf_op jit(solution)/shard_map/ppermute | solution.py:707
  16.3 4.2 %collective-permute-start.3 = (f32[68,8,128]{2,1,0:T(8,128)S(1)}, f32[68,8,128]{2,1,0:T(8,128)S(1)}, u32[]{:S(2)}, u32[]{:S(2)}) collective-permute-start(f32[68,8,128]{2,1,0:T(8,128)S(1)} %get-tuple-element.32), channel_id=1, source_target_pairs={{0,1},{2,3},{4,5},{6,7},{8,9},{10,11},{12,13},{14,15},{1,0},{3,2},... | collective-permute-start | bytes 835592 | tf_op jit(solution)/shard_map/ppermute | solution.py:708
  67.4 12.1 %collective-permute-start.4 = (f32[1280,128]{1,0:T(8,128)S(1)}, f32[1280,128]{1,0:T(8,128)S(1)}, u32[]{:S(2)}, u32[]{:S(2)}) collective-permute-start(f32[1280,128]{1,0:T(8,128)S(1)} %bitcast.2), channel_id=1, source_target_pairs={{0,1},{1,0},{2,3},{3,2},{4,5},{5,4},{6,7},{7,6},{8,9},{9,8},{10,11... | collective-permute-start | bytes 1966088 | tf_op jit(solution)/shard_map/ppermute | solution.py:713
  73.1 13.7 %collective-permute-start.6 = (f32[2,24,128]{2,1,0:T(8,128)S(1)}, f32[2,24,128]{2,1,0:T(8,128)S(1)}, u32[]{:S(2)}, u32[]{:S(2)}) collective-permute-start(f32[2,24,128]{2,1,0:T(8,128)S(1)} %get-tuple-element.34), channel_id=1, source_target_pairs={{16,32},{48,64},{80,96},{112,128},{144,160},{176,192},{208,224},{2... | collective-permute-start | bytes 73736 | tf_op jit(solution)/shard_map/ppermute | solution.py:715
  73.7 13.1 %collective-permute-start.5 = (f32[2,24,128]{2,1,0:T(8,128)S(1)}, f32[2,24,128]{2,1,0:T(8,128)S(1)}, u32[]{:S(2)}, u32[]{:S(2)}) collective-permute-start(f32[2,24,128]{2,1,0:T(8,128)S(1)} %get-tuple-element.34), channel_id=1, source_target_pairs={{0,16},{32,48},{64,80},{96,112},{128,144},{160,176},{192,208},{224... | collective-permute-start | bytes 73736 | tf_op jit(solution)/shard_map/ppermute | solution.py:714

commit v4 on v3

--- a/solution.py
+++ b/solution.py
@@ -190,9 +190,9 @@
         active[x] = mask
         source[x] = mask * source[x]
 
-    loop(low0, high0, 2, fine_mask)
-
-    face_weights(1.0, coef, wx, wy, wz, low0, high0, 2, 1)
+    loop(low0, high0, 4, fine_mask)
+
+    face_weights(1.0, coef, wx, wy, wz, low0, high0, 4, 1)
 
     def fine_start(x, slot):
         diagonal = diagonal_of(1.0, x, coef, wx, wy, wz, 1)
@@ -201,7 +201,7 @@
         inv[x] = inverse
         update[x] = source[x] * (inverse * inverse_center)
 
-    loop(low0, high0, 2, fine_start)
+    loop(low0, high0, 4, fine_start)
 
     def fine_operate(ref, x):
         return operate(ref[x - 1], ref[x], ref[x + 1], wx[x + 1], wx[x], wy[x], wz[x], diag[x], active[x], 1)
@@ -211,7 +211,7 @@
         first = update[x]
         smooth[x] = first + (carry_weight * first + fresh_weight * residual * inv[x])
 
-    loop(low0 + 1, high0 - 1, 2, fine_finish)
+    loop(low0 + 1, high0 - 1, 3, fine_finish)
 
     def keep(i, slot):
         for kept, ref in (
@@ -221,7 +221,7 @@
             kept[i] = ref[X0 + i, Y0:Y0 + TY, :]
         wx0_ref[i] = wx[X0 + i, Y0:Y0 + TY, :]
 
-    loop(0, TX, 2, keep)
+    loop(0, TX, 4, keep)
 
     def restrict(value, slot):
         pairs[slot] = pair_lanes(value, 1, jnp.add)
@@ -342,25 +342,26 @@
 
     def unpack(refs):
         def body(w, slot):
+            def turned(c, k):
+                return block_transpose(
+                    [
+                        refs[c][pl.ds((q * (wide // 4) + w) * stride + k, deep, stride=ROWS), :]
+                        for q in range(4)
+                    ],
+                    lanes,
+                )
+
+            parts = [[turned(c, k) for k in range(ROWS)] for c in range(2)]
             for c in range(2):
-                def turned(k):
-                    return block_transpose(
-                        [
-                            refs[c][pl.ds((q * (wide // 4) + w) * stride + k, deep, stride=ROWS), :]
-                            for q in range(4)
-                        ],
-                        lanes,
-                    )
-
-                loads, coefs, tops = (turned(0), turned(1)), (turned(2), turned(3)), turned(4)
+                *fields, tops = parts[c]
                 for y in range(4):
                     tall = (
                         jnp.where(low, tops[y], shift(tops[y], 16, 1)),
                         jnp.where(low, shift(tops[y], -16, 1), tops[y]),
                     )
                     for i in range(2):
-                        residual[2 * w + i, 4 * c + y] = loads[i][y]
-                        coef[2 * w + i, 4 * c + y] = coefs[i][y]
+                        residual[2 * w + i, 4 * c + y] = fields[i][y]
+                        coef[2 * w + i, 4 * c + y] = fields[2 + i][y]
                         active[2 * w + i, 4 * c + y] = (layer < tall[i]).astype(F32)
 
         loop(0, planes // 2, 1, body)
@@ -566,7 +567,7 @@
         update0[x] = value
         second0[x] = guess0[x] + value
 
-    loop(1, TX - 1, 2, fine_first)
+    loop(1, TX - 1, 5, fine_first)
     margin = BX - X0
 
     def fine_second(x, slot):
@@ -576,7 +577,7 @@
         )
         out_ref[x - margin] = value[BY - Y0:2 * BY - Y0]
 
-    loop(margin, margin + BX, 2, fine_second)
+    loop(margin, margin + BX, 4, fine_second)
 
 
 def in_vmem(count):

time: 89.3 us -> 87.9 us (0.984)
  Pallas kernels: 16.5 us -> 15.1 us
    pallas_call x1, Pallas kernels: 6.05 us -> 5.03 us  [local_part(): pl.pallas_call(local_kernel, out_shape=outs, in_specs=in_vmem(5), out_spe...]
where the time goes in v4:
time: 87.9 us; the launch traced here: 87.5 us
  blocking collectives  40.8 us (46%)
  starting transfers between devices  27.1 us (31%)
  Pallas kernels  15.1 us (17%)
  waiting for transfers between devices  4.46 us (5%)
    all_to_all x1, blocking collectives, shards(): mine = lax.all_to_all(fan, ('wide', 'z'), 0, 0, tiled=True)  40.8 us
    pallas_call x1, Pallas kernels, coarse_part(): pl.pallas_call(functools.partial(coarse_kernel, wide, deep), out_shape=ja...  7.21 us
    ppermute x1, starting transfers between devices, shards(): even = lax.ppermute(even, 'wide', swapped(wide, 0))  6.56 us
    ppermute x1, starting transfers between devices, shards(): even = lax.ppermute(edge, 'wide', swapped(wide, 0))  5.81 us
    ppermute x1, starting transfers between devices, shards(): far = lax.ppermute(far, ('z', 'core'), swapped(2 * deep, 1))  5.8 us
    ppermute x1, starting transfers between devices, shards(): other = lax.ppermute(mine, 'core', [(0, 1), (1, 0)])  5.63 us
    pallas_call x1, Pallas kernels, local_part(): pl.pallas_call(local_kernel, out_shape=outs, in_specs=in_vmem(5), out_spe...  5.03 us
    ppermute x1, waiting for transfers between devices, shards(): far = lax.ppermute(far, ('z', 'core'), swapped(2 * deep, 1))  2.29 us
  transfers between devices with their start and end apart: 7, of which 2 were waited for; matrix products, arithmetic and copies ran while one was open for 0% of the time, Pallas kernels for 8%

profile of v4, /device:TPU:1, one launch (start us, length us, event | category | flops | bytes accessed | tf_op | source)
XLA Modules:
  0.0 87.5 jit_solution(14685302746255332399)
XLA Ops:
  0.0 1.0 %pack_part.1 = (f32[17,16,128]{2,1,0:T(8,128)S(1)}, f32[14,16,128]{2,1,0:T(8,128)S(1)}, f32[14,16,128]{2,1,0:T(8,128)S(1)}) custom-call(f32[8,16,128]{2,1,0:T(8,128)} %source_ref.1, f32[8,16,128]{2,1,0:T(8,128)} %coef_ref.1, s32[8,16]{1,0:T(8,128)} %tops_ref.1), custom_call_target="tpu_custom_call" | custom-call | tf_op jit(solution)/shard_map/pack_part/pallas_call | solution.py:692
  1.0 0.7 collective-permute-start
  1.7 6.6 %collective-permute-start.1 = (f32[14,16,128]{2,1,0:T(8,128)S(1)}, f32[14,16,128]{2,1,0:T(8,128)S(1)}, u32[]{:S(2)}, u32[]{:S(2)}) collective-permute-start(f32[14,16,128]{2,1,0:T(8,128)S(1)} %get-tuple-element.30), channel_id=1, source_target_pairs={{0,16},{32,48},{64,80},{96,112},{128,144},{160,176},{192,208},{224... | collective-permute-start | bytes 344072 | tf_op jit(solution)/shard_map/ppermute | solution.py:706
  8.3 0.0 collective-permute-done.left_ref
  8.3 2.2 %collective-permute-done.1.right_ref = f32[14,16,128]{2,1,0:T(8,128)S(1)} collective-permute-done((f32[14,16,128]{2,1,0:T(8,128)S(1)}, f32[14,16,128]{2,1,0:T(8,128)S(1)}, u32[]{:S(2)}, u32[]{:S(2)}) %collective-permute-start.1) | collective-permute-done | bytes 114720 | tf_op jit(solution)/shard_map/ppermute | solution.py:706
  10.4 0.1 strip_part.1
  10.5 5.8 %collective-permute-start.2 = (f32[68,8,128]{2,1,0:T(8,128)S(1)}, f32[68,8,128]{2,1,0:T(8,128)S(1)}, u32[]{:S(2)}, u32[]{:S(2)}) collective-permute-start(f32[68,8,128]{2,1,0:T(8,128)S(1)} %get-tuple-element.31), channel_id=1, source_target_pairs={{1,2},{3,4},{5,6},{7,8},{9,10},{11,12},{13,14},{2,1},{4,3},{6,5},{... | collective-permute-start | bytes 835592 | tf_op jit(solution)/shard_map/ppermute | solution.py:708
  16.3 1.9 %collective-permute-start.3 = (f32[68,8,128]{2,1,0:T(8,128)S(1)}, f32[68,8,128]{2,1,0:T(8,128)S(1)}, u32[]{:S(2)}, u32[]{:S(2)}) collective-permute-start(f32[68,8,128]{2,1,0:T(8,128)S(1)} %get-tuple-element.32), channel_id=1, source_target_pairs={{0,1},{2,3},{4,5},{6,7},{8,9},{10,11},{12,13},{14,15},{1,0},{3,2},... | collective-permute-start | bytes 835592 | tf_op jit(solution)/shard_map/ppermute | solution.py:709
  18.3 2.3 %collective-permute-done.2.far_ref = f32[68,8,128]{2,1,0:T(8,128)S(1)} collective-permute-done((f32[68,8,128]{2,1,0:T(8,128)S(1)}, f32[68,8,128]{2,1,0:T(8,128)S(1)}, u32[]{:S(2)}, u32[]{:S(2)}) %collective-permute-start.2) | collective-permute-done | bytes 278560 | tf_op jit(solution)/shard_map/ppermute | solution.py:708
  20.5 0.0 collective-permute-done.3.near_ref
  20.5 5.0 %local_part.1 = (f32[1280,128]{1,0:T(8,128)S(1)}, f32[2,24,128]{2,1,0:T(8,128)S(1)}, f32[12,24,128]{2,1,0:T(8,128)S(1)}, f32[12,24,128]{2,1,0:T(8,128)S(1)}, f32...) custom-call(f32[17,16,128]{2,1,0:T(8,128)S(1)} %get-tuple-element.28, ...), custom_call_target="tpu_custom_call" | custom-call | tf_op jit(solution)/shard_map/local_part/pallas_call | solution.py:614
  25.6 40.8 %all_to_all.5 = f32[256,1,640]{2,1,0:T(1,128)S(1)} all-to-all(f32[256,1,640]{2,1,0:T(1,128)S(1)} %bitcast.4), channel_id=1, replica_groups=mesh['wide'=32,'z'=8,'core'=2] {'wide','z'}, dimensions={0} | all-to-all | bytes 1310720 | tf_op jit(solution)/shard_map/all_to_all | solution.py:712
  66.4 5.6 %collective-permute-start.4 = (f32[1280,128]{1,0:T(8,128)S(1)}, f32[1280,128]{1,0:T(8,128)S(1)}, u32[]{:S(2)}, u32[]{:S(2)}) collective-permute-start(f32[1280,128]{1,0:T(8,128)S(1)} %bitcast.2), channel_id=1, source_target_pairs={{0,1},{1,0},{2,3},{3,2},{4,5},{5,4},{6,7},{7,6},{8,9},{9,8},{10,11... | collective-permute-start | bytes 1966088 | tf_op jit(solution)/shard_map/ppermute | solution.py:714
  72.0 0.7 collective-permute-start.6
  72.7 5.8 %collective-permute-start.5 = (f32[2,24,128]{2,1,0:T(8,128)S(1)}, f32[2,24,128]{2,1,0:T(8,128)S(1)}, u32[]{:S(2)}, u32[]{:S(2)}) collective-permute-start(f32[2,24,128]{2,1,0:T(8,128)S(1)} %get-tuple-element.34), channel_id=1, source_target_pairs={{0,16},{32,48},{64,80},{96,112},{128,144},{160,176},{192,208},{224... | collective-permute-start | bytes 73736 | tf_op jit(solution)/shard_map/ppermute | solution.py:715
  78.5 0.0 collective-permute-done.4.other_ref
  78.5 7.2 %coarse_part.1.wanted = f32[96,128]{1,0:T(8,128)S(1)} custom-call(f32[1280,128]{1,0:T(8,128)S(1)} %bitcast.3, f32[1280,128]{1,0:T(8,128)S(1)} %collective-permute-done.4.other_ref), custom_call_target="tpu_custom_call" | custom-call | flops 32768000 | bytes 4194304 | tf_op jit(solution)/shard_map/coarse_part/pallas_call | solution.py:631
  85.8 0.0 collective-permute-done.6.odd_ref
  85.8 0.0 collective-permute-done.5.even_ref
  85.8 1.8 %finish_part.1 = f32[8,16,128]{2,1,0:T(8,128)} custom-call(f32[96,128]{1,0:T(8,128)S(1)} %coarse_part.1.wanted, f32[2,24,128]{2,1,0:T(8,128)S(1)} %collective-permute-done.5.even_ref, f32[2,24,128]{2,1,0:T(8,128)S(1)} %collective-permute-done.6.odd_ref, f32[12,24,128]{2,1,0:T(8,128)S(1)} %get-tuple-element.35.load1_ref, ...), custom_call_target="tpu_custom_call" | custom-call | tf_op jit(solution)/shard_map/finish_part/pallas_call | solution.py:645
Async XLA Ops:
  1.0 7.2 %collective-permute-start = (f32[14,16,128]{2,1,0:T(8,128)S(1)}, f32[14,16,128]{2,1,0:T(8,128)S(1)}, u32[]{:S(2)}, u32[]{:S(2)}) collective-permute-start(f32[14,16,128]{2,1,0:T(8,128)S(1)} %get-tuple-element.29), channel_id=1, source_target_pairs={{16,32},{48,64},{80,96},{112,128},{144,160},{176,192},{208,224},{2... | collective-permute-start | bytes 344072 | tf_op jit(solution)/shard_map/ppermute | solution.py:705
  1.7 8.7 %collective-permute-start.1 = (f32[14,16,128]{2,1,0:T(8,128)S(1)}, f32[14,16,128]{2,1,0:T(8,128)S(1)}, u32[]{:S(2)}, u32[]{:S(2)}) collective-permute-start(f32[14,16,128]{2,1,0:T(8,128)S(1)} %get-tuple-element.30), channel_id=1, source_target_pairs={{0,16},{32,48},{64,80},{96,112},{128,144},{160,176},{192,208},{224... | collective-permute-start | bytes 344072 | tf_op jit(solution)/shard_map/ppermute | solution.py:706
  10.5 10.0 %collective-permute-start.2 = (f32[68,8,128]{2,1,0:T(8,128)S(1)}, f32[68,8,128]{2,1,0:T(8,128)S(1)}, u32[]{:S(2)}, u32[]{:S(2)}) collective-permute-start(f32[68,8,128]{2,1,0:T(8,128)S(1)} %get-tuple-element.31), channel_id=1, source_target_pairs={{1,2},{3,4},{5,6},{7,8},{9,10},{11,12},{13,14},{2,1},{4,3},{6,5},{... | collective-permute-start | bytes 835592 | tf_op jit(solution)/shard_map/ppermute | solution.py:708
  16.3 4.2 %collective-permute-start.3 = (f32[68,8,128]{2,1,0:T(8,128)S(1)}, f32[68,8,128]{2,1,0:T(8,128)S(1)}, u32[]{:S(2)}, u32[]{:S(2)}) collective-permute-start(f32[68,8,128]{2,1,0:T(8,128)S(1)} %get-tuple-element.32), channel_id=1, source_target_pairs={{0,1},{2,3},{4,5},{6,7},{8,9},{10,11},{12,13},{14,15},{1,0},{3,2},... | collective-permute-start | bytes 835592 | tf_op jit(solution)/shard_map/ppermute | solution.py:709
  66.4 12.1 %collective-permute-start.4 = (f32[1280,128]{1,0:T(8,128)S(1)}, f32[1280,128]{1,0:T(8,128)S(1)}, u32[]{:S(2)}, u32[]{:S(2)}) collective-permute-start(f32[1280,128]{1,0:T(8,128)S(1)} %bitcast.2), channel_id=1, source_target_pairs={{0,1},{1,0},{2,3},{3,2},{4,5},{5,4},{6,7},{7,6},{8,9},{9,8},{10,11... | collective-permute-start | bytes 1966088 | tf_op jit(solution)/shard_map/ppermute | solution.py:714
  72.0 13.7 %collective-permute-start.6 = (f32[2,24,128]{2,1,0:T(8,128)S(1)}, f32[2,24,128]{2,1,0:T(8,128)S(1)}, u32[]{:S(2)}, u32[]{:S(2)}) collective-permute-start(f32[2,24,128]{2,1,0:T(8,128)S(1)} %get-tuple-element.34), channel_id=1, source_target_pairs={{16,32},{48,64},{80,96},{112,128},{144,160},{176,192},{208,224},{2... | collective-permute-start | bytes 73736 | tf_op jit(solution)/shard_map/ppermute | solution.py:716
  72.7 13.1 %collective-permute-start.5 = (f32[2,24,128]{2,1,0:T(8,128)S(1)}, f32[2,24,128]{2,1,0:T(8,128)S(1)}, u32[]{:S(2)}, u32[]{:S(2)}) collective-permute-start(f32[2,24,128]{2,1,0:T(8,128)S(1)} %get-tuple-element.34), channel_id=1, source_target_pairs={{0,16},{32,48},{64,80},{96,112},{128,144},{160,176},{192,208},{224... | collective-permute-start | bytes 73736 | tf_op jit(solution)/shard_map/ppermute | solution.py:715

commit v5 on v4

--- a/solution.py
+++ b/solution.py
@@ -182,7 +182,7 @@
         layer = (lane_index((MY, BZ)) & ~1).astype(F32)
         active1_ref[x] = (layer < value).astype(F32)
 
-    loop(0, MX, 2, middle_tops)
+    loop(0, MX, 4, middle_tops)
 
     def fine_mask(x, slot):
         layer = lane_index((EY, BZ)).astype(F32)
@@ -230,14 +230,14 @@
     def middle_coef(x, slot):
         coef1[x] = restrict(coef[2 * x] + coef[2 * x + 1], slot) * 0.125
 
-    loop(low1 - 1, high1 + 1, 2, middle_coef)
+    loop(low1 - 1, high1 + 1, 5, middle_coef)
 
     def middle_load(x, slot):
         left = source[2 * x] - fine_operate(smooth, 2 * x)
         right = source[2 * x + 1] - fine_operate(smooth, 2 * x + 1)
         load1_ref[x] = restrict(left + right, slot)
 
-    loop(low1, high1, 2, middle_load)
+    loop(low1, high1, 4, middle_load)
 
     face_weights(2.0, coef1, wx1_ref, wy1_ref, wz1_ref, low1, high1, 4, 2)
 
@@ -616,7 +616,7 @@
         out_shape=outs,
         in_specs=in_vmem(5),
         out_specs=in_vmem(len(outs)),
-        scratch_shapes=big + scratch(2, MX, MY, BZ) + scratch(1, 2, EY, BZ)
+        scratch_shapes=big + scratch(2, MX, MY, BZ) + scratch(1, 5, EY, BZ)
         + scratch(1, MX, MY, BZ) + scratch(1, MY, BZ),
         compiler_params=pltpu.CompilerParams(vmem_limit_bytes=24 * 2**20),
         name="local_part",

time: 87.9 us -> 87.4 us (level)
  no operation moved by 1% of the time
where the time goes in v5:
time: 87.4 us; the launch traced here: 87.1 us
  blocking collectives  40.8 us (47%)
  starting transfers between devices  27.1 us (31%)
  Pallas kernels  14.6 us (17%)
  waiting for transfers between devices  4.46 us (5%)
    all_to_all x1, blocking collectives, shards(): mine = lax.all_to_all(fan, ('wide', 'z'), 0, 0, tiled=True)  40.8 us
    pallas_call x1, Pallas kernels, coarse_part(): pl.pallas_call(functools.partial(coarse_kernel, wide, deep), out_shape=ja...  7.21 us
    ppermute x1, starting transfers between devices, shards(): even = lax.ppermute(even, 'wide', swapped(wide, 0))  6.56 us
    ppermute x1, starting transfers between devices, shards(): even = lax.ppermute(edge, 'wide', swapped(wide, 0))  5.81 us
    ppermute x1, starting transfers between devices, shards(): far = lax.ppermute(far, ('z', 'core'), swapped(2 * deep, 1))  5.8 us
    ppermute x1, starting transfers between devices, shards(): other = lax.ppermute(mine, 'core', [(0, 1), (1, 0)])  5.63 us
    pallas_call x1, Pallas kernels, local_part(): pl.pallas_call(local_kernel, out_shape=outs, in_specs=in_vmem(5), out_spe...  4.57 us
    ppermute x1, waiting for transfers between devices, shards(): far = lax.ppermute(far, ('z', 'core'), swapped(2 * deep, 1))  2.29 us
  transfers between devices with their start and end apart: 7, of which 2 were waited for; matrix products, arithmetic and copies ran while one was open for 0% of the time, Pallas kernels for 8%

profile of v5, /device:TPU:1, one launch (start us, length us, event | category | flops | bytes accessed | tf_op | source)
XLA Modules:
  0.0 87.1 jit_solution(10760547378390094271)
XLA Ops:
  0.0 1.0 %pack_part.1 = (f32[17,16,128]{2,1,0:T(8,128)S(1)}, f32[14,16,128]{2,1,0:T(8,128)S(1)}, f32[14,16,128]{2,1,0:T(8,128)S(1)}) custom-call(f32[8,16,128]{2,1,0:T(8,128)} %source_ref.1, f32[8,16,128]{2,1,0:T(8,128)} %coef_ref.1, s32[8,16]{1,0:T(8,128)} %tops_ref.1), custom_call_target="tpu_custom_call" | custom-call | tf_op jit(solution)/shard_map/pack_part/pallas_call | solution.py:692
  1.0 0.7 collective-permute-start
  1.7 6.6 %collective-permute-start.1 = (f32[14,16,128]{2,1,0:T(8,128)S(1)}, f32[14,16,128]{2,1,0:T(8,128)S(1)}, u32[]{:S(2)}, u32[]{:S(2)}) collective-permute-start(f32[14,16,128]{2,1,0:T(8,128)S(1)} %get-tuple-element.30), channel_id=1, source_target_pairs={{0,16},{32,48},{64,80},{96,112},{128,144},{160,176},{192,208},{224... | collective-permute-start | bytes 344072 | tf_op jit(solution)/shard_map/ppermute | solution.py:706
  8.3 0.0 collective-permute-done.left_ref
  8.3 2.2 %collective-permute-done.1.right_ref = f32[14,16,128]{2,1,0:T(8,128)S(1)} collective-permute-done((f32[14,16,128]{2,1,0:T(8,128)S(1)}, f32[14,16,128]{2,1,0:T(8,128)S(1)}, u32[]{:S(2)}, u32[]{:S(2)}) %collective-permute-start.1) | collective-permute-done | bytes 114720 | tf_op jit(solution)/shard_map/ppermute | solution.py:706
  10.4 0.1 strip_part.1
  10.5 5.8 %collective-permute-start.2 = (f32[68,8,128]{2,1,0:T(8,128)S(1)}, f32[68,8,128]{2,1,0:T(8,128)S(1)}, u32[]{:S(2)}, u32[]{:S(2)}) collective-permute-start(f32[68,8,128]{2,1,0:T(8,128)S(1)} %get-tuple-element.31), channel_id=1, source_target_pairs={{1,2},{3,4},{5,6},{7,8},{9,10},{11,12},{13,14},{2,1},{4,3},{6,5},{... | collective-permute-start | bytes 835592 | tf_op jit(solution)/shard_map/ppermute | solution.py:708
  16.3 1.9 %collective-permute-start.3 = (f32[68,8,128]{2,1,0:T(8,128)S(1)}, f32[68,8,128]{2,1,0:T(8,128)S(1)}, u32[]{:S(2)}, u32[]{:S(2)}) collective-permute-start(f32[68,8,128]{2,1,0:T(8,128)S(1)} %get-tuple-element.32), channel_id=1, source_target_pairs={{0,1},{2,3},{4,5},{6,7},{8,9},{10,11},{12,13},{14,15},{1,0},{3,2},... | collective-permute-start | bytes 835592 | tf_op jit(solution)/shard_map/ppermute | solution.py:709
  18.3 2.3 %collective-permute-done.2.far_ref = f32[68,8,128]{2,1,0:T(8,128)S(1)} collective-permute-done((f32[68,8,128]{2,1,0:T(8,128)S(1)}, f32[68,8,128]{2,1,0:T(8,128)S(1)}, u32[]{:S(2)}, u32[]{:S(2)}) %collective-permute-start.2) | collective-permute-done | bytes 278560 | tf_op jit(solution)/shard_map/ppermute | solution.py:708
  20.5 0.0 collective-permute-done.3.near_ref
  20.5 4.6 %local_part.1 = (f32[1280,128]{1,0:T(8,128)S(1)}, f32[2,24,128]{2,1,0:T(8,128)S(1)}, f32[12,24,128]{2,1,0:T(8,128)S(1)}, f32[12,24,128]{2,1,0:T(8,128)S(1)}, f32...) custom-call(f32[17,16,128]{2,1,0:T(8,128)S(1)} %get-tuple-element.28, ...), custom_call_target="tpu_custom_call" | custom-call | tf_op jit(solution)/shard_map/local_part/pallas_call | solution.py:614
  25.1 40.8 %all_to_all.5 = f32[256,1,640]{2,1,0:T(1,128)S(1)} all-to-all(f32[256,1,640]{2,1,0:T(1,128)S(1)} %bitcast.4), channel_id=1, replica_groups=mesh['wide'=32,'z'=8,'core'=2] {'wide','z'}, dimensions={0} | all-to-all | bytes 1310720 | tf_op jit(solution)/shard_map/all_to_all | solution.py:712
  65.9 5.6 %collective-permute-start.4 = (f32[1280,128]{1,0:T(8,128)S(1)}, f32[1280,128]{1,0:T(8,128)S(1)}, u32[]{:S(2)}, u32[]{:S(2)}) collective-permute-start(f32[1280,128]{1,0:T(8,128)S(1)} %bitcast.2), channel_id=1, source_target_pairs={{0,1},{1,0},{2,3},{3,2},{4,5},{5,4},{6,7},{7,6},{8,9},{9,8},{10,11... | collective-permute-start | bytes 1966088 | tf_op jit(solution)/shard_map/ppermute | solution.py:714
  71.6 0.7 collective-permute-start.6
  72.2 5.8 %collective-permute-start.5 = (f32[2,24,128]{2,1,0:T(8,128)S(1)}, f32[2,24,128]{2,1,0:T(8,128)S(1)}, u32[]{:S(2)}, u32[]{:S(2)}) collective-permute-start(f32[2,24,128]{2,1,0:T(8,128)S(1)} %get-tuple-element.34), channel_id=1, source_target_pairs={{0,16},{32,48},{64,80},{96,112},{128,144},{160,176},{192,208},{224... | collective-permute-start | bytes 73736 | tf_op jit(solution)/shard_map/ppermute | solution.py:715
  78.1 0.0 collective-permute-done.4.other_ref
  78.1 7.2 %coarse_part.1.wanted = f32[96,128]{1,0:T(8,128)S(1)} custom-call(f32[1280,128]{1,0:T(8,128)S(1)} %bitcast.3, f32[1280,128]{1,0:T(8,128)S(1)} %collective-permute-done.4.other_ref), custom_call_target="tpu_custom_call" | custom-call | flops 32768000 | bytes 4194304 | tf_op jit(solution)/shard_map/coarse_part/pallas_call | solution.py:631
  85.3 0.0 collective-permute-done.6.odd_ref
  85.3 0.0 collective-permute-done.5.even_ref
  85.3 1.8 %finish_part.1 = f32[8,16,128]{2,1,0:T(8,128)} custom-call(f32[96,128]{1,0:T(8,128)S(1)} %coarse_part.1.wanted, f32[2,24,128]{2,1,0:T(8,128)S(1)} %collective-permute-done.5.even_ref, f32[2,24,128]{2,1,0:T(8,128)S(1)} %collective-permute-done.6.odd_ref, f32[12,24,128]{2,1,0:T(8,128)S(1)} %get-tuple-element.35.load1_ref, ...), custom_call_target="tpu_custom_call" | custom-call | tf_op jit(solution)/shard_map/finish_part/pallas_call | solution.py:645
Async XLA Ops:
  1.0 7.2 %collective-permute-start = (f32[14,16,128]{2,1,0:T(8,128)S(1)}, f32[14,16,128]{2,1,0:T(8,128)S(1)}, u32[]{:S(2)}, u32[]{:S(2)}) collective-permute-start(f32[14,16,128]{2,1,0:T(8,128)S(1)} %get-tuple-element.29), channel_id=1, source_target_pairs={{16,32},{48,64},{80,96},{112,128},{144,160},{176,192},{208,224},{2... | collective-permute-start | bytes 344072 | tf_op jit(solution)/shard_map/ppermute | solution.py:705
  1.7 8.7 %collective-permute-start.1 = (f32[14,16,128]{2,1,0:T(8,128)S(1)}, f32[14,16,128]{2,1,0:T(8,128)S(1)}, u32[]{:S(2)}, u32[]{:S(2)}) collective-permute-start(f32[14,16,128]{2,1,0:T(8,128)S(1)} %get-tuple-element.30), channel_id=1, source_target_pairs={{0,16},{32,48},{64,80},{96,112},{128,144},{160,176},{192,208},{224... | collective-permute-start | bytes 344072 | tf_op jit(solution)/shard_map/ppermute | solution.py:706
  10.5 10.0 %collective-permute-start.2 = (f32[68,8,128]{2,1,0:T(8,128)S(1)}, f32[68,8,128]{2,1,0:T(8,128)S(1)}, u32[]{:S(2)}, u32[]{:S(2)}) collective-permute-start(f32[68,8,128]{2,1,0:T(8,128)S(1)} %get-tuple-element.31), channel_id=1, source_target_pairs={{1,2},{3,4},{5,6},{7,8},{9,10},{11,12},{13,14},{2,1},{4,3},{6,5},{... | collective-permute-start | bytes 835592 | tf_op jit(solution)/shard_map/ppermute | solution.py:708
  16.3 4.2 %collective-permute-start.3 = (f32[68,8,128]{2,1,0:T(8,128)S(1)}, f32[68,8,128]{2,1,0:T(8,128)S(1)}, u32[]{:S(2)}, u32[]{:S(2)}) collective-permute-start(f32[68,8,128]{2,1,0:T(8,128)S(1)} %get-tuple-element.32), channel_id=1, source_target_pairs={{0,1},{2,3},{4,5},{6,7},{8,9},{10,11},{12,13},{14,15},{1,0},{3,2},... | collective-permute-start | bytes 835592 | tf_op jit(solution)/shard_map/ppermute | solution.py:709
  65.9 12.1 %collective-permute-start.4 = (f32[1280,128]{1,0:T(8,128)S(1)}, f32[1280,128]{1,0:T(8,128)S(1)}, u32[]{:S(2)}, u32[]{:S(2)}) collective-permute-start(f32[1280,128]{1,0:T(8,128)S(1)} %bitcast.2), channel_id=1, source_target_pairs={{0,1},{1,0},{2,3},{3,2},{4,5},{5,4},{6,7},{7,6},{8,9},{9,8},{10,11... | collective-permute-start | bytes 1966088 | tf_op jit(solution)/shard_map/ppermute | solution.py:714
  71.6 13.7 %collective-permute-start.6 = (f32[2,24,128]{2,1,0:T(8,128)S(1)}, f32[2,24,128]{2,1,0:T(8,128)S(1)}, u32[]{:S(2)}, u32[]{:S(2)}) collective-permute-start(f32[2,24,128]{2,1,0:T(8,128)S(1)} %get-tuple-element.34), channel_id=1, source_target_pairs={{16,32},{48,64},{80,96},{112,128},{144,160},{176,192},{208,224},{2... | collective-permute-start | bytes 73736 | tf_op jit(solution)/shard_map/ppermute | solution.py:716
  72.2 13.1 %collective-permute-start.5 = (f32[2,24,128]{2,1,0:T(8,128)S(1)}, f32[2,24,128]{2,1,0:T(8,128)S(1)}, u32[]{:S(2)}, u32[]{:S(2)}) collective-permute-start(f32[2,24,128]{2,1,0:T(8,128)S(1)} %get-tuple-element.34), channel_id=1, source_target_pairs={{0,16},{32,48},{64,80},{96,112},{128,144},{160,176},{192,208},{224... | collective-permute-start | bytes 73736 | tf_op jit(solution)/shard_map/ppermute | solution.py:715
